TPU v7x, 256 devices: a whole 4x4x8 slice. The times are simulated.
256 devices in a mesh: tm: 8 (over y, core), vert: 32 (over z, x).
Axes of the slice: x: 4, y: 4, z: 8, core: 2. Of those that a mesh axis runs over, the one named last changes fastest.
Arguments:
- features: bfloat16 [32, 16384, 128], P('tm', 'vert'), may hold values from -6 to 6
- tile_cols: int32 [32, 128, 8], P('tm', 'vert'), may hold values from 0 to 127, as said below
- tile_vals: bfloat16 [32, 128, 8, 128, 128], P('tm', 'vert'), may hold values from -0.1875 to 0.1875
- space_weight: bfloat16 [128, 128], replicated, may hold values from -0.5 to 0.5
- positions: bfloat16 [32, 128], replicated, may hold values from -6 to 6
- attn_proj: bfloat16 [128, 384], replicated, may hold values from -0.5 to 0.5
- attn_out: bfloat16 [128, 128], replicated, may hold values from -0.5 to 0.5
- norm_gain: float32 [128], replicated, may hold values from 0.1 to 1.9
- mlp_up: bfloat16 [128, 512], replicated, may hold values from -0.5 to 0.5
- mlp_down: bfloat16 [512, 128], replicated, may hold values from -0.25 to 0.25
Outputs:
- embedded: bfloat16 [32, 16384, 128], P('tm', 'vert')
Inputs may be any that keep to these rules, and one draw needn't show every extreme that they name: `tile_cols`: for each snapshot and each group of 4 consecutive row blocks, the listed column blocks name at most two distinct blocks among those of any one group (blocks c with the same c // 4), and exactly two for some group.
All inputs are finite; a program needn't handle non-finite values.
Results may differ from a plain program's by a relative error of at most 0.0064.
Values may be sent and summed in bfloat16 or wider, within the bound.
A program may use at most 128 MiB of HBM per device.

v0:
```python
import math

import jax
import jax.numpy as jnp
from jax import lax
from jax.sharding import PartitionSpec as P

HEADS = 16


cap_value = 4.0
norm_eps = 1e-05


def temporal(hidden, positions, attn_proj, attn_out, norm_gain, mlp_up, mlp_down):
    snap_total = hidden.shape[0]
    feature_dim = hidden.shape[2]
    head_count = HEADS
    head_dim = feature_dim // head_count
    mixed_in = (hidden.astype(jnp.float32) + positions.astype(jnp.float32)[:, None, :]).astype(
        jnp.bfloat16
    )
    flat_in = mixed_in.reshape(-1, feature_dim)
    projected = jnp.dot(flat_in, attn_proj, preferred_element_type=jnp.float32).astype(jnp.bfloat16)
    projected = projected.reshape(snap_total, -1, 3, head_count, head_dim)
    query_part = projected[:, :, 0]
    key_part = projected[:, :, 1]
    value_part = projected[:, :, 2]
    scores = jnp.einsum(
        "tvhd,uvhd->vhtu", query_part, key_part, preferred_element_type=jnp.float32
    ) / math.sqrt(head_dim)
    capped = cap_value * jnp.tanh(scores / cap_value)
    causal = jnp.arange(snap_total)[:, None] >= jnp.arange(snap_total)[None, :]
    raised = jnp.where(causal, jnp.exp(capped), 0.0)
    weights = (raised / jnp.sum(raised, axis=-1, keepdims=True)).astype(jnp.bfloat16)
    attended = jnp.einsum(
        "vhtu,uvhd->tvhd", weights, value_part, preferred_element_type=jnp.float32
    ).astype(jnp.bfloat16)
    stream = flat_in.astype(jnp.float32) + jnp.dot(
        attended.reshape(-1, feature_dim), attn_out, preferred_element_type=jnp.float32
    )
    centre = jnp.mean(stream, axis=-1, keepdims=True)
    spread = jnp.mean((stream - centre) ** 2, axis=-1, keepdims=True)
    normed = ((stream - centre) * lax.rsqrt(spread + norm_eps) * norm_gain).astype(jnp.bfloat16)
    expanded = jax.nn.relu(jnp.dot(normed, mlp_up, preferred_element_type=jnp.float32)).astype(
        jnp.bfloat16
    )
    output = stream + jnp.dot(expanded, mlp_down, preferred_element_type=jnp.float32)
    return output.astype(jnp.bfloat16).reshape(snap_total, -1, feature_dim)


def spatial(features, tile_cols, tile_vals, space_weight):
    snap_count, row_count, feature_dim = features.shape
    tile_size = tile_vals.shape[-1]
    block_count = row_count // tile_size
    tile_count = tile_cols.shape[2]
    flat_cols = tile_cols.reshape(snap_count, block_count * tile_count)
    everything = lax.all_gather(features, "vert", axis=1, tiled=True)
    everything = everything.reshape(snap_count, -1, tile_size, feature_dim)
    blocks = jnp.take_along_axis(everything, flat_cols[:, :, None, None], axis=1)
    blocks = blocks.reshape(snap_count, block_count, tile_count, tile_size, feature_dim)
    summed = jnp.einsum(
        "srkij,srkjd->srid", tile_vals, blocks, preferred_element_type=jnp.float32
    ).astype(jnp.bfloat16)
    hidden = jax.nn.relu(
        jnp.dot(summed.reshape(-1, feature_dim), space_weight, preferred_element_type=jnp.float32)
    )
    return hidden.astype(jnp.bfloat16).reshape(snap_count, row_count, feature_dim)


def local(
    features,
    tile_cols,
    tile_vals,
    space_weight,
    positions,
    attn_proj,
    attn_out,
    norm_gain,
    mlp_up,
    mlp_down,
):
    snap_count, row_count, feature_dim = features.shape
    time_count = lax.axis_size("tm")
    hidden = spatial(features, tile_cols, tile_vals, space_weight)
    grouped = hidden.reshape(snap_count, time_count, row_count // time_count, feature_dim)
    arrived = lax.all_to_all(grouped, "tm", split_axis=1, concat_axis=0, tiled=True)
    snap_total = arrived.shape[0]
    timeline = arrived.reshape(snap_total, -1, feature_dim)
    result = temporal(timeline, positions, attn_proj, attn_out, norm_gain, mlp_up, mlp_down)
    result = result.reshape(snap_total, 1, -1, feature_dim)
    embedded = lax.all_to_all(result, "tm", split_axis=0, concat_axis=1, tiled=True)
    return embedded.reshape(snap_count, row_count, feature_dim)


def solution(mesh):
    placed = (
        P("tm", "vert", None),
        P("tm", "vert", None),
        P("tm", "vert", None, None, None),
        P(),
        P(),
        P(),
        P(),
        P(),
        P(),
        P(),
    )
    return jax.shard_map(
        local, mesh=mesh, in_specs=placed, out_specs=P("tm", "vert", None), check_vma=False
    )
```

profile of v0, /device:TPU:1, one launch (start us, length us, event | category | flops | bytes accessed | tf_op | source)
XLA Modules:
  0.0 253.4 jit_solution(15430646949209116984)
XLA Ops:
  6.5 0.7 all-gather.2.cloned.1.call-update
  7.3 0.8 broadcast_in_dim_reshape.3
  8.1 0.7 compare_and_fusion
  8.8 143.9 %all-gather.2.cloned.1.call-done = bf16[4,16384,128]{2,1,0:T(8,128)(2,1)} async-done(((bf16[4,512,128]{2,1,0:T(8,128)(2,1)}), bf16[4,16384,128]{2,1,0:T(8,128)(2,1)}) %all-gather.2.cloned.1.call-update) | async-done | bytes 16777232 | tf_op jit(solution)/shard_map/all_gather | solution.py:58
  152.7 8.8 %gather_fusion = bf16[128,128,128]{2,1,0:T(8,128)(2,1)} fusion(bf16[4,128,128,128]{3,2,1,0:T(8,128)(2,1)} %bitcast.66, s32[128]{0:T(128)S(1)} %reshape.115), kind=kCustom, calls=%fused_computation | custom fusion | bytes 8389632 | tf_op jit(solution)/shard_map/jit(take_along_axis)/gather | solution.py:60
  161.6 4.8 %fusion.17 = bf16[4,4,128,128]{2,3,1,0:T(8,128)(2,1)S(1)} fusion(bf16[4,4,8,128,128]{4,3,2,1,0:T(8,128)(2,1)} %param.12, bf16[4,4,8,128,128]{4,3,2,1,0:T(8,128)(2,1)} %bitcast.63, pred[4,4,8]{2,1,0:T(4,128)(4,1)S(1)} %compare_and_fusion), kind=kOutput, calls=%fused_computation.22 | convolution fusion | flops 539230208 | bytes 8913024 | tf_op jit(solution)/shard_map/srkij,srkjd->srid/dot_general | solution.py:62
  166.7 0.8 copy.25
  167.5 5.7 %all-to-all-start = ((bf16[4,8,64,128]{3,2,0,1:T(8,128)(2,1)}), bf16[4,8,64,128]{3,2,0,1:T(8,128)(2,1)S(1)}, u32[]{:S(2)}, u32[]{:S(2)}) async-start(bf16[4,8,64,128]{3,2,0,1:T(8,128)(2,1)} %copy.25), calls=%async_computation | async-start | bytes 1048576 | tf_op jit(solution)/shard_map/all_to_all | solution.py:87
  173.2 9.3 %all-to-all-done = bf16[4,8,64,128]{3,2,0,1:T(8,128)(2,1)S(1)} async-done(((bf16[4,8,64,128]{3,2,0,1:T(8,128)(2,1)}), bf16[4,8,64,128]{3,2,0,1:T(8,128)(2,1)S(1)}, u32[]{:S(2)}, u32[]{:S(2)}) %all-to-all-start) | async-done | bytes 524320 | tf_op jit(solution)/shard_map/all_to_all | solution.py:87
  182.8 0.8 copy-done.1
  184.1 1.7 copy.26
  185.8 4.6 %reshape.110 = bf16[32,64,3,16,8]{1,0,4,3,2:T(8,128)(2,1)S(1)} reshape(bf16[2048,384]{0,1:T(8,128)(2,1)} %copy.26) | data formatting | bytes 3145728 | tf_op jit(solution)/shard_map/reshape | solution.py:25
  190.4 1.8 fusion.35
  192.2 4.3 %copy.37 = bf16[32,64,1,16,8]{0,4,3,1,2:T(8,128)(2,1)S(1)} copy(bf16[32,64,1,16,8]{1,0,4,3,2:T(8,128)(2,1)} %get-tuple-element.6) | data formatting | bytes 1048576
  196.5 4.9 %copy.38 = bf16[32,64,1,16,8]{0,4,3,1,2:T(8,128)(2,1)} copy(bf16[32,64,1,16,8]{1,0,4,3,2:T(8,128)(2,1)} %get-tuple-element.7) | data formatting | bytes 1048576
  201.3 3.9 %copy.36 = bf16[32,64,1,16,8]{0,4,3,1,2:T(8,128)(2,1)} copy(bf16[32,64,1,16,8]{1,0,4,3,2:T(8,128)(2,1)S(1)} %copy-done.3) | data formatting | bytes 1048576
  205.2 11.1 %fusion = (f32[64,16,32]{2,1,0:T(8,128)S(1)}, f32[64,16,32,32]{2,3,1,0:T(8,128)}) fusion(pred[32,32]{0,1:T(8,128)(4,1)S(1)} %iota_compare_fusion, bf16[32,64,1,16,8]{0,4,3,1,2:T(8,128)(2,1)} %copy.38, bf16[32,64,1,16,8]{0,4,3,1,2:T(8,128)(2,1)S(1)} %copy.37), kind=kOutput, calls=%fused_computation.3 | convolution fusion | flops 20938752 | bytes 5374976 | tf_op jit(solution)/shard_map/tvhd,uvhd->vhtu/dot_general | solution.py:29
  216.4 9.8 %convert_bitcast_fusion = bf16[32,64,16,8]{0,3,2,1:T(8,128)(2,1)} fusion(f32[64,16,32,32]{2,3,1,0:T(8,128)} %get-tuple-element.9, f32[64,16,32]{2,1,0:T(8,128)S(1)} %get-tuple-element.8, pred[32,32]{0,1:T(8,128)(4,1)S(1)} %iota_compare_fusion, bf16[32,64,1,16,8]{0,4,3,1,2:T(8,128)(2,1)S(1)} %copy-done.4), kind=kOutput, calls=%fused_computation.19 | convolution fusion | flops 22282240 | bytes 5374976 | tf_op jit(solution)/shard_map/vhtu,uvhd->tvhd/dot_general | solution.py:36
  226.2 3.4 %copy.31 = bf16[32,64,16,8]{1,0,3,2:T(8,128)(2,1)S(1)} copy(bf16[32,64,16,8]{0,3,2,1:T(8,128)(2,1)} %convert_bitcast_fusion) | data formatting | bytes 1048576 | tf_op jit(solution)/shard_map/convert_element_type | solution.py:38
  229.6 0.8 reshape.111
  231.0 0.6 multiply_reduce_fusion
  231.7 1.3 fusion.6
  233.0 12.7 %all_to_all.24 = bf16[32,1,64,128]{3,2,1,0:T(8,128)(2,1)S(1)} all-to-all(bf16[32,1,64,128]{3,2,1,0:T(8,128)(2,1)S(1)} %bitcast.67), channel_id=1, replica_groups=mesh['tm'=8,'vert'=32] {'tm'}, dimensions={0} | all-to-all | bytes 1048576 | tf_op jit(solution)/shard_map/all_to_all | solution.py:92
  245.7 0.8 copy.33
  (33 shorter events, 1.7 us)
Async XLA Ops:
  6.5 225.1 %copy-start = (bf16[512,128]{1,0:T(8,128)(2,1)S(1)}, bf16[512,128]{1,0:T(8,128)(2,1)}, u32[]{:S(2)}) copy-start(bf16[512,128]{1,0:T(8,128)(2,1)} %param.19) | copy-start | bytes 393220
  6.5 146.2 %all-gather.2.cloned.1.call-start = ((), (), s32[]{:S(2)}) async-start(), calls=%async_computation.2 | async-start | bytes 17301504 | tf_op jit(solution)/shard_map/all_gather | solution.py:58
  161.6 4.8 %copy-start.7 = (bf16[128,128]{1,0:T(8,128)(2,1)S(1)}, bf16[128,128]{1,0:T(8,128)(2,1)}, u32[]{:S(2)}) copy-start(bf16[128,128]{1,0:T(8,128)(2,1)} %param.13) | copy-start | bytes 98308
  161.6 11.7 %copy-start.8 = (bf16[32,128]{1,0:T(8,128)(2,1)S(1)}, bf16[32,128]{1,0:T(8,128)(2,1)}, u32[]{:S(2)}) copy-start(bf16[32,128]{1,0:T(8,128)(2,1)} %param.14) | copy-start | bytes 24580
  166.4 17.2 %copy-start.5 = (bf16[128,384]{1,0:T(8,128)(2,1)S(1)}, bf16[128,384]{1,0:T(8,128)(2,1)}, u32[]{:S(2)}) copy-start(bf16[128,384]{1,0:T(8,128)(2,1)} %param.15) | copy-start | bytes 294916
  167.5 15.0 %all-to-all-start = ((bf16[4,8,64,128]{3,2,0,1:T(8,128)(2,1)}), bf16[4,8,64,128]{3,2,0,1:T(8,128)(2,1)S(1)}, u32[]{:S(2)}, u32[]{:S(2)}) async-start(bf16[4,8,64,128]{3,2,0,1:T(8,128)(2,1)} %copy.25), calls=%async_computation | async-start | bytes 1048576 | tf_op jit(solution)/shard_map/all_to_all | solution.py:87
  182.8 0.8 copy-start.1
  192.2 9.1 %copy-start.3 = (bf16[32,64,1,16,8]{1,0,4,3,2:T(8,128)(2,1)S(1)}, bf16[32,64,1,16,8]{1,0,4,3,2:T(8,128)(2,1)}, u32[]{:S(2)}) copy-start(bf16[32,64,1,16,8]{1,0,4,3,2:T(8,128)(2,1)} %get-tuple-element.5) | copy-start | bytes 1572868
  205.2 11.1 %copy-start.4 = (bf16[32,64,1,16,8]{0,4,3,1,2:T(8,128)(2,1)S(1)}, bf16[32,64,1,16,8]{0,4,3,1,2:T(8,128)(2,1)}, u32[]{:S(2)}) copy-start(bf16[32,64,1,16,8]{0,4,3,1,2:T(8,128)(2,1)} %copy.36) | copy-start | bytes 1572868
  226.1 4.2 %copy-start.2 = (bf16[2048,128]{1,0:T(8,128)(2,1)S(1)}, bf16[2048,128]{1,0:T(8,128)(2,1)}, u32[]{:S(2)}) copy-start(bf16[2048,128]{1,0:T(8,128)(2,1)} %copy-done.1) | copy-start | bytes 1572868
  226.1 4.2 %copy-start.6 = (bf16[128,128]{1,0:T(8,128)(2,1)S(1)}, bf16[128,128]{1,0:T(8,128)(2,1)}, u32[]{:S(2)}) copy-start(bf16[128,128]{1,0:T(8,128)(2,1)} %param.16) | copy-start | bytes 98308
  226.2 5.5 %copy-start.9 = (bf16[128,512]{1,0:T(8,128)(2,1)S(1)}, bf16[128,512]{1,0:T(8,128)(2,1)}, u32[]{:S(2)}) copy-start(bf16[128,512]{1,0:T(8,128)(2,1)} %param.18) | copy-start | bytes 393220
  226.2 5.5 %copy-start.10 = (f32[128]{0:T(128)S(1)}, f32[128]{0:T(128)}, u32[]{:S(2)}) copy-start(f32[128]{0:T(128)} %param.17) | copy-start | bytes 1540
Sparse Core Ops, SparseCore 0:
  9.9 142.7 all-gather.1
where the time goes:
time: 254 us; the launch traced here: 253 us
  waiting for transfers between devices  154 us (61%)
  local copies, waits for them, and re-layouts  37.5 us (15%)
  matrix products  28.4 us (11%)
  between operations  13.6 us (5%)
  blocking collectives  12.7 us (5%)
  starting transfers between devices  5.69 us (2%)
    all_gather x1, waiting for transfers between devices, spatial(): everything = lax.all_gather(features, 'vert', axis=1, tiled=True)  144 us
    unnamed x25, local copies, waits for them, and re-layouts  13.9 us
    all_to_all x1, blocking collectives, local(): lax.all_to_all(result, 'tm', split_axis=0, concat_axis=1, tiled=True)  12.7 us
    dot_general x1, matrix products, temporal(): jnp.einsum('tvhd,uvhd->vhtu', query_part, key_part, preferred_element_typ...  11.1 us
    dot_general x1, matrix products, temporal(): jnp.einsum('vhtu,uvhd->tvhd', weights, value_part, preferred_element_type...  9.77 us
    all_to_all x1, waiting for transfers between devices, local(): lax.all_to_all(grouped, 'tm', split_axis=1, concat_axis=0, tiled=True)  9.33 us
    gather x2, local copies, waits for them, and re-layouts, spatial(): jnp.take_along_axis(everything, flat_cols[:, :, None, None], axis=1)  8.93 us
    all_to_all x1, starting transfers between devices, local(): lax.all_to_all(grouped, 'tm', split_axis=1, concat_axis=0, tiled=True)  5.69 us
  transfers between devices with their start and end apart: 2, of which 2 were waited for; matrix products, arithmetic and copies ran while one was open for 1% of the time, Pallas kernels for 0%

commit v1 on v0

--- a/solution.py
+++ b/solution.py
@@ -1,15 +1,23 @@
+import functools
 import math
 
 import jax
 import jax.numpy as jnp
 from jax import lax
+from jax.experimental import pallas as pl
+from jax.experimental.pallas import tpu as pltpu
 from jax.sharding import PartitionSpec as P
 
 HEADS = 16
-
-
+MESH = pl.DeviceIdType.MESH
 cap_value = 4.0
 norm_eps = 1e-05
+
+ZORD = (0, 1, 7, 2, 6, 3, 5, 4)
+POS = {dz: p for p, dz in enumerate(ZORD)}
+GROUPS = ((0,), (1, 7), (2, 6), (3, 5), (4,))
+PAIRED = (0, 1, 2)
+DIRECT = (3,)
 
 
 def temporal(hidden, positions, attn_proj, attn_out, norm_gain, mlp_up, mlp_down):
@@ -49,48 +57,216 @@
     return output.astype(jnp.bfloat16).reshape(snap_total, -1, feature_dim)
 
 
+class Sems:
+    def __init__(self, send, recv):
+        self.send, self.recv, self.n = send, recv, 0
+
+    def copy(self, src, dst, device):
+        i = self.n
+        self.n += 1
+        return pltpu.make_async_remote_copy(
+            src, dst, self.send.at[i], self.recv.at[i], device_id=device, device_id_type=MESH
+        )
+
+
+COPIES = 3 + 4 * 8 + len(PAIRED) * 9 + 5 * (4 * 2 + len(DIRECT)) + 4 * 7
+
+
+def spatial_kernel(
+    feat, tab_s, tab_v, slots, weight, tv_hbm, out,
+    tv, tabr, tabs, stg, hid, arr, send, recv, lsem, *bufs,
+):
+    bufs = list(bufs)
+    comp = [bufs.pop(0) for _ in range(4)]
+    own = [{dz: bufs.pop(0) for dz in range(1, 8)} for _ in range(4)]
+    pair = {s: {dz: bufs.pop(0) for dz in range(8)} for s in PAIRED}
+    for s in range(4):
+        own[s][0] = feat.at[s]
+
+    v = lax.axis_index("vert")
+    t = lax.axis_index("tm")
+    z, x = v // 4, v % 4
+    up = dict(vert=((z + 1) % 8) * 4 + x)
+    down = dict(vert=((z + 7) % 8) * 4 + x)
+    side = {k: dict(vert=z * 4 + (x + k) % 4) for k in (1, 2, 3)}
+    times = {k: dict(tm=(t + k) % 8) for k in range(1, 8)}
+
+    barrier = pltpu.get_barrier_semaphore()
+    peers = [up, down] + list(side.values()) + list(times.values())
+    for peer in peers:
+        pl.semaphore_signal(barrier, inc=1, device_id=peer, device_id_type=MESH)
+    pl.semaphore_wait(barrier, len(peers))
+
+    sems = Sems(send, recv)
+    started = []
+
+    def go(copy):
+        copy.start()
+        started.append(copy)
+        return copy
+
+    def ring(buf, step):
+        if step < 4:
+            a = sems.copy(buf[(9 - step) % 8], buf[8 - step], up)
+            b = sems.copy(buf[step - 1], buf[step], down)
+        else:
+            a = sems.copy(buf[5].at[0:2], buf[4].at[0:2], up)
+            b = sems.copy(buf[3].at[2:4], buf[4].at[2:4], down)
+        return go(a), go(b)
+
+    tables = {k: go(sems.copy(tab_v, tabr.at[3 - k], side[k])) for k in (1, 2, 3)}
+    load = pltpu.make_async_copy(tv_hbm, tv, lsem.at[0])
+    load.start()
+    ringed = {s: ring(own[s], 1) for s in range(4)}
+    swapped = {s: go(sems.copy(feat.at[s], pair[s][0], side[2])) for s in PAIRED}
+    for k in (1, 2, 3):
+        tables[k].wait_recv()
+    for k in (1, 2, 3):
+        pltpu.make_async_copy(tabr.at[k - 1], tabs.at[k - 1], lsem.at[k]).start()
+    for k in (1, 2, 3):
+        pltpu.make_async_copy(tabr.at[k - 1], tabs.at[k - 1], lsem.at[k]).wait()
+
+    stg_refs = stg
+    stg = {}
+    n = 0
+    for s in range(4):
+        for k in (1, 3) if s in PAIRED else (1, 3, 2):
+            stg[s, k] = stg_refs.at[n]
+            n += 1
+    crossed = {s: [] for s in range(4)}
+
+    def keep(buf, s, dx, group):
+        for dz in group:
+            ci = dx * 8 + POS[dz]
+            for w in range(2):
+                comp[s][ci * 2 + w] = buf[dz][tab_s[s, w * 32 + ci]]
+
+    def share(s, group):
+        p0 = POS[group[0]]
+        rows = 2 * len(group)
+        for k in (1, 3) if s in PAIRED else (1, 3, 2):
+            ref = stg[s, k]
+            dx = 4 - k
+            for dz in group:
+                for w in range(2):
+                    ci = dx * 8 + POS[dz]
+                    ref[POS[dz] * 2 + w] = own[s][dz][tabs[k - 1, s, w * 32 + ci]]
+        keep(own[s], s, 0, group)
+        for k in (1, 3) if s in PAIRED else (1, 3, 2):
+            dx = 4 - k
+            crossed[s].append(
+                go(
+                    sems.copy(
+                        stg[s, k].at[2 * p0 : 2 * p0 + rows],
+                        comp[s].at[dx * 16 + 2 * p0 : dx * 16 + 2 * p0 + rows],
+                        side[k],
+                    )
+                )
+            )
+
+    for s in range(4):
+        share(s, GROUPS[0])
+    paired = {}
+    for step in range(1, 5):
+        for s in range(4):
+            for c in ringed[s]:
+                c.wait_recv()
+            if step < 4:
+                ringed[s] = ring(own[s], step + 1)
+            if step == 3 and s in PAIRED:
+                swapped[s].wait_recv()
+                paired[s] = ring(pair[s], 1)
+            share(s, GROUPS[step])
+    for s in PAIRED:
+        keep(pair[s], s, 2, GROUPS[0])
+    for step in range(1, 5):
+        for s in PAIRED:
+            for c in paired[s]:
+                c.wait_recv()
+            if step < 4:
+                paired[s] = ring(pair[s], step + 1)
+            keep(pair[s], s, 2, GROUPS[step])
+
+    load.wait()
+    sent = []
+    for s in DIRECT + PAIRED:
+        for c in crossed[s]:
+            c.wait_recv()
+        for r in range(4):
+            left = jnp.concatenate([tv[s, r, k] for k in range(8)], axis=1)
+            right = jnp.concatenate([comp[s][slots[s, r * 8 + k]] for k in range(8)], axis=0)
+            summed = jnp.dot(left, right, preferred_element_type=jnp.float32).astype(jnp.bfloat16)
+            hidden = jnp.dot(summed, weight[...], preferred_element_type=jnp.float32)
+            hidden = jnp.maximum(hidden, 0.0).astype(jnp.bfloat16)
+            hid[s, 2 * r : 2 * r + 2] = hidden.reshape(2, 64, 128)
+        arr[t * 4 + s] = hid[s, t]
+        for k in range(1, 8):
+            c = sems.copy(hid.at[s, (t + k) % 8], arr.at[t * 4 + s], times[k])
+            sent.append(go(c))
+    for c in sent:
+        c.wait_recv()
+    out[...] = arr[...]
+    for c in started:
+        c.wait_send()
+    assert sems.n == COPIES
+
+
 def spatial(features, tile_cols, tile_vals, space_weight):
-    snap_count, row_count, feature_dim = features.shape
-    tile_size = tile_vals.shape[-1]
-    block_count = row_count // tile_size
-    tile_count = tile_cols.shape[2]
-    flat_cols = tile_cols.reshape(snap_count, block_count * tile_count)
-    everything = lax.all_gather(features, "vert", axis=1, tiled=True)
-    everything = everything.reshape(snap_count, -1, tile_size, feature_dim)
-    blocks = jnp.take_along_axis(everything, flat_cols[:, :, None, None], axis=1)
-    blocks = blocks.reshape(snap_count, block_count, tile_count, tile_size, feature_dim)
-    summed = jnp.einsum(
-        "srkij,srkjd->srid", tile_vals, blocks, preferred_element_type=jnp.float32
-    ).astype(jnp.bfloat16)
-    hidden = jax.nn.relu(
-        jnp.dot(summed.reshape(-1, feature_dim), space_weight, preferred_element_type=jnp.float32)
-    )
-    return hidden.astype(jnp.bfloat16).reshape(snap_count, row_count, feature_dim)
+    v = lax.axis_index("vert")
+    z, x = v // 4, v % 4
+    cols = tile_cols.reshape(4, 32)
+    owner, blk = cols // 4, cols % 4
+    dz, dx = (owner // 4 - z) % 8, (owner % 4 - x) % 4
+    pos = jnp.where(dz == 0, 0, jnp.where(dz <= 4, 2 * dz - 1, 2 * (8 - dz)))
+    ci = dx * 8 + pos
+    hit = ci[:, :, None] == jnp.arange(32)
+    low = jnp.min(jnp.where(hit, blk[:, :, None], 3), axis=1)
+    high = jnp.max(jnp.where(hit, blk[:, :, None], 0), axis=1)
+    mine = jnp.sum(jnp.where(hit, low[:, None, :], 0), axis=2)
+    slots = ci * 2 + (blk != mine).astype(jnp.int32)
+    table = jnp.pad(jnp.concatenate([low, high], axis=1), ((0, 4), (0, 64)))
+
+    vmem = pl.BlockSpec(memory_space=pltpu.VMEM)
+    smem = pl.BlockSpec(memory_space=pltpu.SMEM)
+    blocks = functools.partial(pltpu.VMEM, dtype=jnp.bfloat16)
+    block4 = pltpu.VMEM((4, 128, 128), jnp.bfloat16)
+    stages = 2 * 4 + len(DIRECT)
+    return pl.pallas_call(
+        spatial_kernel,
+        out_shape=jax.ShapeDtypeStruct((32, 64, 128), jnp.bfloat16),
+        in_specs=[vmem, smem, vmem, smem, vmem, pl.BlockSpec(memory_space=pl.ANY)],
+        out_specs=vmem,
+        scratch_shapes=[
+            pltpu.VMEM((4, 4, 8, 128, 128), jnp.bfloat16),
+            pltpu.VMEM((3, 8, 128), jnp.int32),
+            pltpu.SMEM((3, 8, 128), jnp.int32),
+            pltpu.VMEM((stages, 16, 128, 128), jnp.bfloat16),
+            pltpu.VMEM((4, 8, 64, 128), jnp.bfloat16),
+            pltpu.VMEM((32, 64, 128), jnp.bfloat16),
+            pltpu.SemaphoreType.DMA((COPIES,)),
+            pltpu.SemaphoreType.DMA((COPIES,)),
+            pltpu.SemaphoreType.DMA((4,)),
+        ]
+        + [pltpu.VMEM((64, 128, 128), jnp.bfloat16)] * 4
+        + [block4] * 28
+        + [block4] * (8 * len(PAIRED)),
+        compiler_params=pltpu.CompilerParams(
+            collective_id=0, has_side_effects=True, vmem_limit_bytes=60 * 2**20
+        ),
+    )(
+        features.reshape(4, 4, 128, 128), table, table, slots, space_weight, tile_vals
+    )
 
 
 def local(
-    features,
-    tile_cols,
-    tile_vals,
-    space_weight,
-    positions,
-    attn_proj,
-    attn_out,
-    norm_gain,
-    mlp_up,
-    mlp_down,
+    features, tile_cols, tile_vals, space_weight, positions, attn_proj, attn_out, norm_gain,
+    mlp_up, mlp_down,
 ):
-    snap_count, row_count, feature_dim = features.shape
-    time_count = lax.axis_size("tm")
-    hidden = spatial(features, tile_cols, tile_vals, space_weight)
-    grouped = hidden.reshape(snap_count, time_count, row_count // time_count, feature_dim)
-    arrived = lax.all_to_all(grouped, "tm", split_axis=1, concat_axis=0, tiled=True)
-    snap_total = arrived.shape[0]
-    timeline = arrived.reshape(snap_total, -1, feature_dim)
+    timeline = spatial(features, tile_cols, tile_vals, space_weight)
     result = temporal(timeline, positions, attn_proj, attn_out, norm_gain, mlp_up, mlp_down)
-    result = result.reshape(snap_total, 1, -1, feature_dim)
+    result = result.reshape(32, 1, -1, 128)
     embedded = lax.all_to_all(result, "tm", split_axis=0, concat_axis=1, tiled=True)
-    return embedded.reshape(snap_count, row_count, feature_dim)
+    return embedded.reshape(4, 512, 128)
 
 
 def solution(mesh):

time: 254 us -> 164 us (0.65)
  waiting for transfers between devices: 154 us -> 0 us
  Pallas kernels: 0 us -> 95.8 us
  between operations: 13.6 us -> 0.17 us
  local copies, waits for them, and re-layouts: 37.5 us -> 28.8 us
  starting transfers between devices: 5.69 us -> 0 us
  matrix products: 28.4 us -> 23.3 us
    all_gather x1 -> x0, waiting for transfers between devices: 144 us -> none  [spatial(): everything = lax.all_gather(features, 'vert', axis=1, tiled=True)]
    pallas_call x0 -> x1, Pallas kernels: none -> 95.8 us  [spatial(): pl.pallas_call(spatial_kernel, out_shape=jax.ShapeDtypeStruct((32, 64, 12...]
    all_to_all x1 -> x0, waiting for transfers between devices: 9.33 us -> none  [local(): lax.all_to_all(grouped, 'tm', split_axis=1, concat_axis=0, tiled=True)]
    gather x2 -> x0, local copies, waits for them, and re-layouts: 8.93 us -> none  [spatial(): jnp.take_along_axis(everything, flat_cols[:, :, None, None], axis=1)]
    all_to_all x1 -> x0, starting transfers between devices: 5.69 us -> none  [local(): lax.all_to_all(grouped, 'tm', split_axis=1, concat_axis=0, tiled=True)]
    dot_general x2 -> x0, matrix products: 5.09 us -> none  [the longest x1 4.81 us: spatial(): jnp.einsum('srkij,srkjd->srid', tile_vals, blocks, preferred_element_type...]
    unnamed x25 -> x21, local copies, waits for them, and re-layouts: 13.9 us -> 13.9 us
  transfers between devices with their start and end apart: 2 -> 0, of which waited for: 2 -> 0; matrix products, arithmetic and copies ran while one was open for 1% -> 0% of each run, Pallas kernels for 0% -> 0%
where the time goes in v1:
time: 164 us
  Pallas kernels  95.8 us (58%)
  local copies, waits for them, and re-layouts  28.8 us (18%)
  matrix products  23.3 us (14%)
  blocking collectives  12.1 us (7%)
  other arithmetic  3.6 us (2%)
    pallas_call x1, Pallas kernels, spatial(): pl.pallas_call(spatial_kernel, out_shape=jax.ShapeDtypeStruct((32, 64, 12...  95.8 us
    unnamed x21, local copies, waits for them, and re-layouts  13.9 us
    all_to_all x1, blocking collectives, local(): lax.all_to_all(result, 'tm', split_axis=0, concat_axis=1, tiled=True)  12.1 us
    dot_general x1, matrix products, temporal(): jnp.einsum('tvhd,uvhd->vhtu', query_part, key_part, preferred_element_typ...  11.1 us
    dot_general x1, matrix products, temporal(): jnp.einsum('vhtu,uvhd->tvhd', weights, value_part, preferred_element_type...  9.79 us
    reshape x1, local copies, waits for them, and re-layouts, temporal(): projected = projected.reshape(snap_total, -1, 3, head_count, head_dim)  4.57 us
    convert_element_type x1, local copies, waits for them, and re-layouts, temporal(): attended = jnp.einsum('vhtu,uvhd->tvhd', weights, value_part, preferred_e...  3.61 us

profile of v1, /device:TPU:1, one launch (start us, length us, event | category | flops | bytes accessed | tf_op | source)
XLA Modules:
  0.0 163.8 jit_solution(13221824644208308264)
XLA Ops:
  0.0 0.8 reshape.145
  1.0 0.2 select_reduce_fusion
  1.2 0.6 convert_add_fusion.slots
  1.9 0.6 pad.4.tab_s.tab_v
  2.5 0.7 convert_element_type.38
  3.2 95.8 %shard_map.100 = bf16[32,64,128]{2,1,0:T(8,128)(2,1)} custom-call(bf16[4,4,128,128]{3,2,1,0:T(8,128)(2,1)} %bitcast.41, s32[8,128]{1,0:T(8,128)} %pad.4.tab_s.tab_v, s32[8,128]{1,0:T(8,128)} %pad.4.tab_s.tab_v, s32[4,32]{1,0:T(4,128)} %convert_add_fusion.slots, bf16[128,128]{1,0:T(8,128)(2,1)} %weight.1, bf16[4,4,8,128,128]{4,3,2,1,0:T(8,128)(2,1)} %tv_hbm.1), custom_call_target="tpu_custom_call" | custom-call | tf_op jit(solution)/shard_map/pallas_call | solution.py:234
  99.0 1.2 add_convert_fusion
  100.2 0.8 copy-done.1
  101.0 0.6 convolution_convert_fusion
  101.6 1.8 %copy.31 = bf16[2048,384]{0,1:T(8,128)(2,1)} copy(bf16[2048,384]{1,0:T(8,128)(2,1)S(1)} %convolution_convert_fusion) | data formatting | bytes 3145728 | tf_op jit(solution)/shard_map/convert_element_type | solution.py:32
  103.4 4.6 %reshape.147 = bf16[32,64,3,16,8]{1,0,4,3,2:T(8,128)(2,1)S(1)} reshape(bf16[2048,384]{0,1:T(8,128)(2,1)} %copy.31) | data formatting | bytes 3145728 | tf_op jit(solution)/shard_map/reshape | solution.py:33
  108.0 1.8 %fusion.28 = (bf16[32,64,1,16,8]{1,0,4,3,2:T(8,128)(2,1)}, bf16[32,64,1,16,8]{1,0,4,3,2:T(8,128)(2,1)}, bf16[32,64,1,16,8]{1,0,4,3,2:T(8,128)(2,1)}) fusion(bf16[32,64,3,16,8]{1,0,4,3,2:T(8,128)(2,1)S(1)} %reshape.147), kind=kLoop, calls=%fused_computation.61 | loop fusion | bytes 3145728 | tf_op jit(solution)/shard_map/slice | solution.py:36
  109.8 4.3 %copy.41 = bf16[32,64,1,16,8]{0,4,3,1,2:T(8,128)(2,1)S(1)} copy(bf16[32,64,1,16,8]{1,0,4,3,2:T(8,128)(2,1)} %get-tuple-element.8) | data formatting | bytes 1048576
  114.1 4.9 %copy.42 = bf16[32,64,1,16,8]{0,4,3,1,2:T(8,128)(2,1)} copy(bf16[32,64,1,16,8]{1,0,4,3,2:T(8,128)(2,1)} %get-tuple-element.9) | data formatting | bytes 1048576
  119.0 3.9 %copy.40 = bf16[32,64,1,16,8]{0,4,3,1,2:T(8,128)(2,1)} copy(bf16[32,64,1,16,8]{1,0,4,3,2:T(8,128)(2,1)S(1)} %copy-done.3) | data formatting | bytes 1048576
  122.9 11.1 %fusion = (f32[64,16,32]{2,1,0:T(8,128)S(1)}, f32[64,16,32,32]{2,3,1,0:T(8,128)}) fusion(pred[32,32]{0,1:T(8,128)(4,1)S(1)} %iota_compare_fusion.1, bf16[32,64,1,16,8]{0,4,3,1,2:T(8,128)(2,1)} %copy.42, bf16[32,64,1,16,8]{0,4,3,1,2:T(8,128)(2,1)S(1)} %copy.41), kind=kOutput, calls=%fused_computation.2 | convolution fusion | flops 20938752 | bytes 5374976 | tf_op jit(solution)/shard_map/tvhd,uvhd->vhtu/dot_general | solution.py:37
  134.0 9.8 %convert_bitcast_fusion = bf16[32,64,16,8]{0,3,2,1:T(8,128)(2,1)} fusion(f32[64,16,32,32]{2,3,1,0:T(8,128)} %get-tuple-element.13, f32[64,16,32]{2,1,0:T(8,128)S(1)} %get-tuple-element.12, pred[32,32]{0,1:T(8,128)(4,1)S(1)} %iota_compare_fusion.1, bf16[32,64,1,16,8]{0,4,3,1,2:T(8,128)(2,1)S(1)} %copy-done.4), kind=kOutput, calls=%fused_computation.13 | convolution fusion | flops 22282240 | bytes 5374976 | tf_op jit(solution)/shard_map/vhtu,uvhd->tvhd/dot_general | solution.py:44
  143.8 3.6 %copy.36 = bf16[32,64,16,8]{1,0,3,2:T(8,128)(2,1)S(1)} copy(bf16[32,64,16,8]{0,3,2,1:T(8,128)(2,1)} %convert_bitcast_fusion) | data formatting | bytes 1048576 | tf_op jit(solution)/shard_map/convert_element_type | solution.py:46
  147.4 0.8 reshape.148
  148.2 0.6 fusion.29
  148.8 0.6 multiply_reduce_fusion
  149.5 1.3 fusion.2
  150.8 12.1 %all_to_all.15 = bf16[32,1,64,128]{3,2,1,0:T(8,128)(2,1)S(1)} all-to-all(bf16[32,1,64,128]{3,2,1,0:T(8,128)(2,1)S(1)} %bitcast.42), channel_id=1, replica_groups=mesh['tm'=8,'vert'=32] {'tm'}, dimensions={0} | all-to-all | bytes 1048576 | tf_op jit(solution)/shard_map/all_to_all | solution.py:268
  162.9 0.8 copy.38
  (23 shorter events, 0.3 us)
Async XLA Ops:
  0.0 149.5 %copy-start = (bf16[512,128]{1,0:T(8,128)(2,1)S(1)}, bf16[512,128]{1,0:T(8,128)(2,1)}, u32[]{:S(2)}) copy-start(bf16[512,128]{1,0:T(8,128)(2,1)} %param.19) | copy-start | bytes 393220
  0.0 101.0 %copy-start.5 = (bf16[128,384]{1,0:T(8,128)(2,1)S(1)}, bf16[128,384]{1,0:T(8,128)(2,1)}, u32[]{:S(2)}) copy-start(bf16[128,384]{1,0:T(8,128)(2,1)} %param.15) | copy-start | bytes 294916
  100.2 0.8 copy-start.1
  109.8 9.2 %copy-start.3 = (bf16[32,64,1,16,8]{1,0,4,3,2:T(8,128)(2,1)S(1)}, bf16[32,64,1,16,8]{1,0,4,3,2:T(8,128)(2,1)}, u32[]{:S(2)}) copy-start(bf16[32,64,1,16,8]{1,0,4,3,2:T(8,128)(2,1)} %get-tuple-element.7) | copy-start | bytes 1572868
  122.9 11.1 %copy-start.4 = (bf16[32,64,1,16,8]{0,4,3,1,2:T(8,128)(2,1)S(1)}, bf16[32,64,1,16,8]{0,4,3,1,2:T(8,128)(2,1)}, u32[]{:S(2)}) copy-start(bf16[32,64,1,16,8]{0,4,3,1,2:T(8,128)(2,1)} %copy.40) | copy-start | bytes 1572868
  143.8 4.4 %copy-start.2 = (bf16[32,64,128]{2,1,0:T(8,128)(2,1)S(1)}, bf16[32,64,128]{2,1,0:T(8,128)(2,1)}, u32[]{:S(2)}) copy-start(bf16[32,64,128]{2,1,0:T(8,128)(2,1)} %copy-done.1) | copy-start | bytes 1572868
  143.8 4.4 %copy-start.6 = (bf16[128,128]{1,0:T(8,128)(2,1)S(1)}, bf16[128,128]{1,0:T(8,128)(2,1)}, u32[]{:S(2)}) copy-start(bf16[128,128]{1,0:T(8,128)(2,1)} %param.16) | copy-start | bytes 98308
  143.8 5.7 %copy-start.7 = (bf16[128,512]{1,0:T(8,128)(2,1)S(1)}, bf16[128,512]{1,0:T(8,128)(2,1)}, u32[]{:S(2)}) copy-start(bf16[128,512]{1,0:T(8,128)(2,1)} %param.18) | copy-start | bytes 393220
  143.8 5.7 %copy-start.8 = (f32[128]{0:T(128)S(1)}, f32[128]{0:T(128)}, u32[]{:S(2)}) copy-start(f32[128]{0:T(128)} %param.17) | copy-start | bytes 1540

commit v2 on v1

--- a/solution.py
+++ b/solution.py
@@ -1,4 +1,3 @@
-import functools
 import math
 
 import jax
@@ -8,10 +7,10 @@
 from jax.experimental.pallas import tpu as pltpu
 from jax.sharding import PartitionSpec as P
 
-HEADS = 16
 MESH = pl.DeviceIdType.MESH
-cap_value = 4.0
 norm_eps = 1e-05
+SCORE = 1.0 / (4.0 * math.sqrt(8.0))
+POWER = 4.0 * math.log2(math.e)
 
 ZORD = (0, 1, 7, 2, 6, 3, 5, 4)
 POS = {dz: p for p, dz in enumerate(ZORD)}
@@ -20,41 +19,90 @@
 DIRECT = (3,)
 
 
-def temporal(hidden, positions, attn_proj, attn_out, norm_gain, mlp_up, mlp_down):
-    snap_total = hidden.shape[0]
-    feature_dim = hidden.shape[2]
-    head_count = HEADS
-    head_dim = feature_dim // head_count
-    mixed_in = (hidden.astype(jnp.float32) + positions.astype(jnp.float32)[:, None, :]).astype(
-        jnp.bfloat16
+def dot_t(a, b):
+    return lax.dot_general(a, b, (((1,), (1,)), ((), ())), preferred_element_type=jnp.float32)
+
+
+def dot(a, b):
+    return jnp.dot(a, b, preferred_element_type=jnp.float32)
+
+
+def arrange(attn_proj, attn_out, wcat, wout):
+    row = lax.broadcasted_iota(jnp.int32, (192, 384), 0)
+    col = lax.broadcasted_iota(jnp.int32, (192, 384), 1)
+    base = (row // 64) * 128 + (row % 8) * 8 + (row // 8) % 8
+    for half in range(2):
+        pick = (col == base + half * 64).astype(jnp.bfloat16)
+        wcat[:, half * 128 : (half + 1) * 128] = dot_t(pick, attn_proj[...]).astype(jnp.bfloat16)
+    row = lax.broadcasted_iota(jnp.int32, (64, 128), 0)
+    col = lax.broadcasted_iota(jnp.int32, (64, 128), 1)
+    base = (row % 8) * 8 + row // 8
+    for half in range(2):
+        pick = (col == base + half * 64).astype(jnp.bfloat16)
+        wout[:, half * 128 : (half + 1) * 128] = dot(pick, attn_out[...]).astype(jnp.bfloat16)
+
+
+def project(t0, t1, arr, pos, wcat, mix, proj):
+    zero = jnp.zeros((64, 128), jnp.bfloat16)
+    rows = []
+    for t in (t0, t1):
+        m = (arr[t].astype(jnp.float32) + pos[t].astype(jnp.float32)).astype(jnp.bfloat16)
+        mix[t] = m
+        rows.append(jnp.concatenate([m, zero], axis=1))
+        rows.append(jnp.concatenate([zero, m], axis=1))
+    both = jnp.concatenate(rows, axis=0)
+    p = dot_t(wcat[...], both).astype(jnp.bfloat16).astype(jnp.float32)
+    for i, t in enumerate((t0, t1)):
+        q = p[:, i * 128 : (i + 1) * 128]
+        proj[t, 0:64] = q[0:64] * SCORE
+        proj[t, 64:192] = q[64:192]
+
+
+def attend(tb, proj, att):
+    def parts(t, k):
+        return proj[t, 64 * k : 64 * (k + 1)].reshape(8, 8, 128)
+
+    for pair in range(2):
+        qs = [parts(4 * tb + 2 * pair + i, 0) for i in range(2)]
+
+        def quad(uq, carry, diag):
+            carry = list(carry)
+            for ui in range(4):
+                if diag and ui > 2 * pair + 1:
+                    continue
+                u = 4 * uq + ui
+                k, v = parts(u, 1), parts(u, 2)
+                for i in range(2):
+                    if diag and ui > 2 * pair + i:
+                        continue
+                    e = jnp.exp2(POWER * jnp.tanh(jnp.sum(qs[i] * k, axis=0)))
+                    carry[2 * i] = carry[2 * i] + e[None] * v
+                    carry[2 * i + 1] = carry[2 * i + 1] + e
+            return tuple(carry)
+
+        zero = (jnp.zeros((8, 8, 128), jnp.float32), jnp.zeros((8, 128), jnp.float32)) * 2
+        carry = lax.fori_loop(0, tb, lambda uq, c: quad(uq, c, False), zero)
+        carry = quad(tb, carry, True)
+        for i in range(2):
+            a = carry[2 * i] * (1.0 / carry[2 * i + 1])[None]
+            att[2 * pair + i] = a.reshape(64, 128)
+
+
+def finish(tb, att, mix, wout, gain, mlp_up, mlp_down):
+    rows = jnp.concatenate([att[i].T for i in range(4)], axis=0).astype(jnp.bfloat16)
+    o = dot(rows, wout[...])
+    out = jnp.concatenate(
+        [o[128 * i : 128 * i + 64, 0:128] + o[128 * i + 64 : 128 * i + 128, 128:256] for i in range(4)],
+        axis=0,
     )
-    flat_in = mixed_in.reshape(-1, feature_dim)
-    projected = jnp.dot(flat_in, attn_proj, preferred_element_type=jnp.float32).astype(jnp.bfloat16)
-    projected = projected.reshape(snap_total, -1, 3, head_count, head_dim)
-    query_part = projected[:, :, 0]
-    key_part = projected[:, :, 1]
-    value_part = projected[:, :, 2]
-    scores = jnp.einsum(
-        "tvhd,uvhd->vhtu", query_part, key_part, preferred_element_type=jnp.float32
-    ) / math.sqrt(head_dim)
-    capped = cap_value * jnp.tanh(scores / cap_value)
-    causal = jnp.arange(snap_total)[:, None] >= jnp.arange(snap_total)[None, :]
-    raised = jnp.where(causal, jnp.exp(capped), 0.0)
-    weights = (raised / jnp.sum(raised, axis=-1, keepdims=True)).astype(jnp.bfloat16)
-    attended = jnp.einsum(
-        "vhtu,uvhd->tvhd", weights, value_part, preferred_element_type=jnp.float32
-    ).astype(jnp.bfloat16)
-    stream = flat_in.astype(jnp.float32) + jnp.dot(
-        attended.reshape(-1, feature_dim), attn_out, preferred_element_type=jnp.float32
-    )
+    m = mix[pl.ds(4 * tb, 4)].reshape(256, 128)
+    stream = m.astype(jnp.float32) + out
     centre = jnp.mean(stream, axis=-1, keepdims=True)
-    spread = jnp.mean((stream - centre) ** 2, axis=-1, keepdims=True)
-    normed = ((stream - centre) * lax.rsqrt(spread + norm_eps) * norm_gain).astype(jnp.bfloat16)
-    expanded = jax.nn.relu(jnp.dot(normed, mlp_up, preferred_element_type=jnp.float32)).astype(
-        jnp.bfloat16
-    )
-    output = stream + jnp.dot(expanded, mlp_down, preferred_element_type=jnp.float32)
-    return output.astype(jnp.bfloat16).reshape(snap_total, -1, feature_dim)
+    shifted = stream - centre
+    spread = jnp.mean(shifted * shifted, axis=-1, keepdims=True)
+    normed = (shifted * lax.rsqrt(spread + norm_eps) * gain[...]).astype(jnp.bfloat16)
+    expanded = jnp.maximum(dot(normed, mlp_up[...]), 0.0).astype(jnp.bfloat16)
+    return (stream + dot(expanded, mlp_down[...])).astype(jnp.bfloat16).reshape(4, 64, 128)
 
 
 class Sems:
@@ -69,12 +117,14 @@
         )
 
 
-COPIES = 3 + 4 * 8 + len(PAIRED) * 9 + 5 * (4 * 2 + len(DIRECT)) + 4 * 7
-
-
-def spatial_kernel(
-    feat, tab_s, tab_v, slots, weight, tv_hbm, out,
-    tv, tabr, tabs, stg, hid, arr, send, recv, lsem, *bufs,
+COPIES = 3 + 4 * 8 + len(PAIRED) * 9 + 5 * (4 * 2 + len(DIRECT)) + 4 * 7 + 7
+
+
+def kernel(
+    feat, tab_s, tab_v, slots, weight, tv_hbm, positions, attn_proj, attn_out, gain, mlp_up,
+    mlp_down, out,
+    tv, tabr, tabs, stg, hid, arr, wcat, wout, pos, mix, proj, att, obuf, oarr, send, recv, lsem,
+    *bufs,
 ):
     bufs = list(bufs)
     comp = [bufs.pop(0) for _ in range(4)]
@@ -133,6 +183,8 @@
         for k in (1, 3) if s in PAIRED else (1, 3, 2):
             stg[s, k] = stg_refs.at[n]
             n += 1
+    arrange(attn_proj, attn_out, wcat, wout)
+    pos[...] = positions[...].astype(jnp.float32).reshape(32, 1, 128)
     crossed = {s: [] for s in range(4)}
 
     def keep(buf, s, dx, group):
@@ -205,13 +257,46 @@
             sent.append(go(c))
     for c in sent:
         c.wait_recv()
-    out[...] = arr[...]
+
+    @pl.loop(0, 16)
+    def _(i):
+        project(2 * i, 2 * i + 1, arr, pos, wcat, mix, proj)
+
+    def back(j):
+        return pltpu.make_async_remote_copy(
+            obuf.at[j], oarr.at[:, t], send.at[sems.n + j], recv.at[sems.n + j],
+            device_id=dict(tm=(t + 1 + j) % 8), device_id_type=MESH,
+        )
+
+    @pl.loop(0, 7)
+    def _(j):
+        tb = (t + 1 + j) % 8
+        attend(tb, proj, att)
+        obuf[j] = finish(tb, att, mix, wout, gain, mlp_up, mlp_down)
+        back(j).start()
+
+    attend(t, proj, att)
+    oarr[:, t] = finish(t, att, mix, wout, gain, mlp_up, mlp_down)
+
+    @pl.loop(0, 7)
+    def _(j):
+        back(j).wait_recv()
+
+    out[...] = oarr[...]
+
+    @pl.loop(0, 7)
+    def _(j):
+        back(j).wait_send()
+
     for c in started:
         c.wait_send()
-    assert sems.n == COPIES
-
-
-def spatial(features, tile_cols, tile_vals, space_weight):
+    assert sems.n + 7 == COPIES
+
+
+def local(
+    features, tile_cols, tile_vals, space_weight, positions, attn_proj, attn_out, norm_gain,
+    mlp_up, mlp_down,
+):
     v = lax.axis_index("vert")
     z, x = v // 4, v % 4
     cols = tile_cols.reshape(4, 32)
@@ -228,13 +313,12 @@
 
     vmem = pl.BlockSpec(memory_space=pltpu.VMEM)
     smem = pl.BlockSpec(memory_space=pltpu.SMEM)
-    blocks = functools.partial(pltpu.VMEM, dtype=jnp.bfloat16)
     block4 = pltpu.VMEM((4, 128, 128), jnp.bfloat16)
     stages = 2 * 4 + len(DIRECT)
-    return pl.pallas_call(
-        spatial_kernel,
-        out_shape=jax.ShapeDtypeStruct((32, 64, 128), jnp.bfloat16),
-        in_specs=[vmem, smem, vmem, smem, vmem, pl.BlockSpec(memory_space=pl.ANY)],
+    embedded = pl.pallas_call(
+        kernel,
+        out_shape=jax.ShapeDtypeStruct((4, 8, 64, 128), jnp.bfloat16),
+        in_specs=[vmem, smem, vmem, smem, vmem, pl.BlockSpec(memory_space=pl.ANY)] + [vmem] * 6,
         out_specs=vmem,
         scratch_shapes=[
             pltpu.VMEM((4, 4, 8, 128, 128), jnp.bfloat16),
@@ -243,6 +327,14 @@
             pltpu.VMEM((stages, 16, 128, 128), jnp.bfloat16),
             pltpu.VMEM((4, 8, 64, 128), jnp.bfloat16),
             pltpu.VMEM((32, 64, 128), jnp.bfloat16),
+            pltpu.VMEM((192, 256), jnp.bfloat16),
+            pltpu.VMEM((64, 256), jnp.bfloat16),
+            pltpu.VMEM((32, 1, 128), jnp.float32),
+            pltpu.VMEM((32, 64, 128), jnp.bfloat16),
+            pltpu.VMEM((32, 192, 128), jnp.float32),
+            pltpu.VMEM((4, 64, 128), jnp.float32),
+            pltpu.VMEM((7, 4, 64, 128), jnp.bfloat16),
+            pltpu.VMEM((4, 8, 64, 128), jnp.bfloat16),
             pltpu.SemaphoreType.DMA((COPIES,)),
             pltpu.SemaphoreType.DMA((COPIES,)),
             pltpu.SemaphoreType.DMA((4,)),
@@ -254,18 +346,9 @@
             collective_id=0, has_side_effects=True, vmem_limit_bytes=60 * 2**20
         ),
     )(
-        features.reshape(4, 4, 128, 128), table, table, slots, space_weight, tile_vals
+        features.reshape(4, 4, 128, 128), table, table, slots, space_weight, tile_vals,
+        positions, attn_proj, attn_out, norm_gain.reshape(1, 128), mlp_up, mlp_down,
     )
-
-
-def local(
-    features, tile_cols, tile_vals, space_weight, positions, attn_proj, attn_out, norm_gain,
-    mlp_up, mlp_down,
-):
-    timeline = spatial(features, tile_cols, tile_vals, space_weight)
-    result = temporal(timeline, positions, attn_proj, attn_out, norm_gain, mlp_up, mlp_down)
-    result = result.reshape(32, 1, -1, 128)
-    embedded = lax.all_to_all(result, "tm", split_axis=0, concat_axis=1, tiled=True)
     return embedded.reshape(4, 512, 128)
 
 

time: 164 us -> 116 us (0.71)
  local copies, waits for them, and re-layouts: 28.8 us -> 3.24 us
  matrix products: 23.3 us -> 0 us
  Pallas kernels: 95.8 us -> 111 us
  blocking collectives: 12.1 us -> 0 us
  other arithmetic: 3.6 us -> 1.06 us
    dot_general x5 -> x0, matrix products: 23.3 us -> none  [the longest x1 11.1 us: temporal(): jnp.einsum('tvhd,uvhd->vhtu', query_part, key_part, preferred_element_typ...]
    pallas_call x1, Pallas kernels: 95.8 us -> 111 us  [local(): pl.pallas_call(kernel, out_shape=jax.ShapeDtypeStruct((4, 8, 64, 128), jn...]
    all_to_all x1 -> x0, blocking collectives: 12.1 us -> none  [local(): lax.all_to_all(result, 'tm', split_axis=0, concat_axis=1, tiled=True)]
    unnamed x21 -> x1, local copies, waits for them, and re-layouts: 13.9 us -> 1.87 us
    reshape x3 -> x1, local copies, waits for them, and re-layouts: 6.21 us -> 0.78 us  [local(): cols = tile_cols.reshape(4, 32)]
    convert_element_type x2 -> x0, local copies, waits for them, and re-layouts: 5.43 us -> none  [the longest x1 3.61 us: temporal(): attended = jnp.einsum('vhtu,uvhd->tvhd', weights, value_part, preferred_e...]
    convert_element_type x2 -> x0, other arithmetic: 1.89 us -> none  [the longest x1 1.19 us: temporal(): (hidden.astype(jnp.float32) + positions.astype(jnp.float32)[:, None, :])....]
    slice x1 -> x0, local copies, waits for them, and re-layouts: 1.81 us -> none  [temporal(): value_part = projected[:, :, 2]]
where the time goes in v2:
time: 116 us; the launch traced here: 115 us
  Pallas kernels  111 us (96%)
  local copies, waits for them, and re-layouts  3.24 us (3%)
    pallas_call x1, Pallas kernels, local(): pl.pallas_call(kernel, out_shape=jax.ShapeDtypeStruct((4, 8, 64, 128), jn...  111 us

profile of v2, /device:TPU:1, one launch (start us, length us, event | category | flops | bytes accessed | tf_op | source)
XLA Modules:
  0.0 115.4 jit_solution(1952335658792805748)
XLA Ops:
  0.0 0.8 reshape.123
  0.8 0.1 select_reduce_fusion.2
  0.9 0.1 pad_add_fusion
  1.0 0.2 select_reduce_fusion
  1.2 0.6 convert_add_fusion.slots
  1.8 0.6 pad.4.tab_s.tab_v
  2.4 111.1 %shard_map.100 = bf16[4,8,64,128]{3,2,1,0:T(8,128)(2,1)} custom-call(bf16[4,4,128,128]{3,2,1,0:T(8,128)(2,1)} %bitcast.4, s32[8,128]{1,0:T(8,128)} %pad.4.tab_s.tab_v, s32[8,128]{1,0:T(8,128)} %pad.4.tab_s.tab_v, s32[4,32]{1,0:T(4,128)} %convert_add_fusion.slots, bf16[128,128]{1,0:T(8,128)(2,1)} %weight.1, bf16[4,4,8,128,128]{4,3,2,1,0:T(8,128)(2,1)} %tv_hbm.1, ...), custom_call_target="tpu_custom_call" | custom-call | tf_op jit(solution)/shard_map/pallas_call | solution.py:318
  113.5 1.9 %copy.12 = bf16[4,512,128]{2,1,0:T(8,128)(2,1)} copy(bf16[4,512,128]{2,1,0:T(8,128)(2,1)} %bitcast.3) | data formatting | bytes 1048576
  (1 shorter events, 0.0 us)

commit v3 on v2

v3 whole, which is shorter than its diff:
```python
import math

import jax
import jax.numpy as jnp
from jax import lax
from jax.experimental import pallas as pl
from jax.experimental.pallas import tpu as pltpu
from jax.sharding import PartitionSpec as P

MESH = pl.DeviceIdType.MESH
norm_eps = 1e-05
SCORE = 1.0 / (4.0 * math.sqrt(8.0))
POWER = 4.0 * math.log2(math.e)

ZORD = (0, 1, 7, 2, 6, 3, 5, 4)
POS = {dz: p for p, dz in enumerate(ZORD)}
GROUPS = ((0,), (1, 7), (2, 6), (3, 5), (4,))
PAIRED = (0, 1, 2)
DIRECT = (3,)
EARLY, LATE = (0,), (1, 2)
ORDER = (3, 0, 1, 2)


def dot_t(a, b):
    return lax.dot_general(a, b, (((1,), (1,)), ((), ())), preferred_element_type=jnp.float32)


def dot(a, b):
    return jnp.dot(a, b, preferred_element_type=jnp.float32)


def arrange(attn_proj, attn_out, wcat, wout):
    row = lax.broadcasted_iota(jnp.int32, (192, 384), 0)
    col = lax.broadcasted_iota(jnp.int32, (192, 384), 1)
    base = (row // 64) * 128 + (row % 8) * 8 + (row // 8) % 8
    for half in range(2):
        pick = (col == base + half * 64).astype(jnp.bfloat16)
        wcat[:, half * 128 : (half + 1) * 128] = dot_t(pick, attn_proj[...]).astype(jnp.bfloat16)
    row = lax.broadcasted_iota(jnp.int32, (64, 128), 0)
    col = lax.broadcasted_iota(jnp.int32, (64, 128), 1)
    base = (row % 8) * 8 + row // 8
    for half in range(2):
        pick = (col == base + half * 64).astype(jnp.bfloat16)
        wout[:, half * 128 : (half + 1) * 128] = dot(pick, attn_out[...]).astype(jnp.bfloat16)


def project(t0, t1, arr, pos, wcat, mix, proj):
    zero = jnp.zeros((64, 128), jnp.bfloat16)
    rows = []
    for t in (t0, t1):
        m = (arr[t].astype(jnp.float32) + pos[t]).astype(jnp.bfloat16)
        mix[t] = m
        rows.append(jnp.concatenate([m, zero], axis=1))
        rows.append(jnp.concatenate([zero, m], axis=1))
    both = jnp.concatenate(rows, axis=0)
    p = dot_t(wcat[...], both).astype(jnp.bfloat16).astype(jnp.float32)
    for i, t in enumerate((t0, t1)):
        q = p[:, i * 128 : (i + 1) * 128]
        proj[t, 0:64] = q[0:64] * SCORE
        proj[t, 64:192] = q[64:192]


def attend(tb, proj, att, slot=0):
    def parts(t, k):
        return proj[t, 64 * k : 64 * (k + 1)].reshape(8, 8, 128)

    for pair in range(2):
        qs = [parts(4 * tb + 2 * pair + i, 0) for i in range(2)]

        def quad(uq, carry, diag):
            carry = list(carry)
            for ui in range(4):
                if diag and ui > 2 * pair + 1:
                    continue
                u = 4 * uq + ui
                k, v = parts(u, 1), parts(u, 2)
                for i in range(2):
                    if diag and ui > 2 * pair + i:
                        continue
                    e = jnp.exp2(POWER * jnp.tanh(jnp.sum(qs[i] * k, axis=0)))
                    carry[2 * i] = carry[2 * i] + e[None] * v
                    carry[2 * i + 1] = carry[2 * i + 1] + e
            return tuple(carry)

        zero = (jnp.zeros((8, 8, 128), jnp.float32), jnp.zeros((8, 128), jnp.float32)) * 2
        carry = lax.fori_loop(0, tb, lambda uq, c: quad(uq, c, False), zero)
        carry = quad(tb, carry, True)
        for i in range(2):
            a = carry[2 * i] * (1.0 / carry[2 * i + 1])[None]
            att[slot + 2 * pair + i] = a.reshape(64, 128)


def finish(blocks, att, mix, wout, gain, mlp_up, mlp_down):
    n = 4 * len(blocks)
    rows = jnp.concatenate([att[i].T for i in range(n)], axis=0).astype(jnp.bfloat16)
    o = dot(rows, wout[...])
    out = jnp.concatenate(
        [o[128 * i : 128 * i + 64, 0:128] + o[128 * i + 64 : 128 * i + 128, 128:256] for i in range(n)],
        axis=0,
    )
    m = jnp.concatenate([mix[pl.ds(4 * tb, 4)].reshape(256, 128) for tb in blocks], axis=0)
    stream = m.astype(jnp.float32) + out
    centre = jnp.mean(stream, axis=-1, keepdims=True)
    shifted = stream - centre
    spread = jnp.mean(shifted * shifted, axis=-1, keepdims=True)
    normed = (shifted * lax.rsqrt(spread + norm_eps) * gain[...]).astype(jnp.bfloat16)
    expanded = jnp.maximum(dot(normed, mlp_up[...]), 0.0).astype(jnp.bfloat16)
    done = (stream + dot(expanded, mlp_down[...])).astype(jnp.bfloat16)
    return done.reshape(len(blocks), 4, 64, 128)


def index_tables(z, x, cols, tab_v, slots_v):
    c = cols[...]
    lane = lax.broadcasted_iota(jnp.int32, (4, 4, 128), 2)
    tab = jnp.where(lane < 32, 3, 0)
    seen = []
    for k in range(8):
        ck = jnp.broadcast_to(c[:, :, k : k + 1], (4, 4, 128))
        blk = ck & 3
        dz = ((ck >> 4) - z) & 7
        dx = ((ck >> 2) - x) & 3
        pos = jnp.where(dz == 0, 0, jnp.where(dz <= 4, 2 * dz - 1, 16 - 2 * dz))
        ci = dx * 8 + pos
        seen.append((blk, ci))
        tab = jnp.where(
            ci == lane,
            jnp.minimum(tab, blk),
            jnp.where(ci + 32 == lane, jnp.maximum(tab, blk), tab),
        )
    low = jnp.min(tab, axis=1, keepdims=True)
    high = jnp.max(tab, axis=1, keepdims=True)
    tab = jnp.where(lane[:, 0:1] < 32, low, high)
    tab_v[...] = jnp.zeros((8, 128), jnp.int32)
    for s in range(4):
        tab_v[s : s + 1] = tab[s]
    slots = jnp.zeros((4, 4, 128), jnp.int32)
    for k, (blk, ci) in enumerate(seen):
        mine = jnp.sum(
            jnp.where(ci == lane, tab.astype(jnp.float32), 0.0), axis=2, keepdims=True
        )
        other = (blk.astype(jnp.float32) != mine).astype(jnp.int32)
        slots = jnp.where(lane == k, 2 * ci + other, slots)
    slots_v[...] = jnp.zeros((4, 8, 128), jnp.int32)
    slots_v[:, 0:4] = slots


class Sems:
    def __init__(self, send, recv):
        self.send, self.recv, self.n = send, recv, 0

    def copy(self, src, dst, device):
        i = self.n
        self.n += 1
        return pltpu.make_async_remote_copy(
            src, dst, self.send.at[i], self.recv.at[i], device_id=device, device_id_type=MESH
        )


COPIES = 3 + 4 * 8 + len(PAIRED) * 9 + 5 * (4 * 2 + len(DIRECT)) + 4 * 7 + 7


def kernel(
    feat_h, cols_h, tv_h, weight_h, positions_h, attn_proj_h, attn_out_h, gain_h, mlp_up_h,
    mlp_down_h, out,
    feat, cols, tv, weight, positions, attn_proj, attn_out, gain, mlp_up, mlp_down,
    tab_v, slots_v, tab_s, slots, tabr, tabs, stg_refs, hid, arr, wcat, wout, pos, mix, proj, att,
    obuf, oarr, send, recv, lsem, *bufs,
):
    bufs = list(bufs)
    comp = [bufs.pop(0) for _ in range(4)]
    own = [{dz: bufs.pop(0) for dz in range(1, 8)} for _ in range(4)]
    pair = {s: {dz: bufs.pop(0) for dz in range(8)} for s in PAIRED}
    for s in range(4):
        own[s][0] = feat.at[s]
    kinds = {s: (1, 3) if s in PAIRED else (1, 3, 2) for s in range(4)}
    stg = {}
    for s in range(4):
        for k in kinds[s]:
            stg[s, k] = stg_refs.at[len(stg)]

    v = lax.axis_index("vert")
    t = lax.axis_index("tm")
    z, x = v // 4, v % 4
    up = dict(vert=((z + 1) % 8) * 4 + x)
    down = dict(vert=((z + 7) % 8) * 4 + x)
    side = {k: dict(vert=z * 4 + (x + k) % 4) for k in (1, 2, 3)}
    times = {k: dict(tm=(t + k) % 8) for k in range(1, 8)}

    barrier = pltpu.get_barrier_semaphore()
    peers = [up, down] + list(side.values()) + list(times.values())
    for peer in peers:
        pl.semaphore_signal(barrier, inc=1, device_id=peer, device_id_type=MESH)

    loads = [
        pltpu.make_async_copy(src, dst, lsem.at[i])
        for i, (src, dst) in enumerate(
            [
                (cols_h, cols), (feat_h, feat), (attn_proj_h, attn_proj), (attn_out_h, attn_out),
                (positions_h, positions), (weight_h, weight), (gain_h, gain), (mlp_up_h, mlp_up),
                (mlp_down_h, mlp_down), (tv_h, tv),
            ]
        )
    ]
    for c in loads:
        c.start()
    loads[0].wait()
    index_tables(z, x, cols, tab_v, slots_v)
    loads[1].wait()
    pl.semaphore_wait(barrier, len(peers))

    sems = Sems(send, recv)
    started = []

    def go(copy):
        copy.start()
        started.append(copy)
        return copy

    def ring(buf, step):
        if step < 4:
            a = sems.copy(buf[(9 - step) % 8], buf[8 - step], up)
            b = sems.copy(buf[step - 1], buf[step], down)
        else:
            a = sems.copy(buf[5].at[0:2], buf[4].at[0:2], up)
            b = sems.copy(buf[3].at[2:4], buf[4].at[2:4], down)
        return go(a), go(b)

    ringed = {}
    ringed[ORDER[0]] = ring(own[ORDER[0]], 1)
    tables = {k: go(sems.copy(tab_v, tabr.at[3 - k], side[k])) for k in (1, 2, 3)}
    for s in ORDER[1:]:
        ringed[s] = ring(own[s], 1)
    swapped = {s: go(sems.copy(feat.at[s], pair[s][0], side[2])) for s in PAIRED}
    for c in loads[2:]:
        c.wait()
    mine = [
        pltpu.make_async_copy(tab_v, tab_s, lsem.at[0]),
        pltpu.make_async_copy(slots_v, slots, lsem.at[1]),
    ]
    for c in mine:
        c.start()
    arrange(attn_proj, attn_out, wcat, wout)
    pos[...] = positions[...].astype(jnp.float32).reshape(32, 1, 128)
    for c in mine:
        c.wait()
    for k in (1, 2, 3):
        tables[k].wait_recv()
    theirs = [pltpu.make_async_copy(tabr.at[k], tabs.at[k], lsem.at[2 + k]) for k in range(3)]
    for c in theirs:
        c.start()
    for c in theirs:
        c.wait()

    crossed = {s: [] for s in range(4)}

    def keep(buf, s, dx, group):
        for dz in group:
            ci = dx * 8 + POS[dz]
            for w in range(2):
                comp[s][ci * 2 + w] = buf[dz][tab_s[s, w * 32 + ci]]

    def share(s, group):
        p0 = POS[group[0]]
        rows = 2 * len(group)
        for k in kinds[s]:
            for dz in group:
                for w in range(2):
                    ci = (4 - k) * 8 + POS[dz]
                    stg[s, k][POS[dz] * 2 + w] = own[s][dz][tabs[k - 1, s, w * 32 + ci]]
        keep(own[s], s, 0, group)
        for k in kinds[s]:
            q = (4 - k) * 16 + 2 * p0
            crossed[s].append(
                go(
                    sems.copy(
                        stg[s, k].at[2 * p0 : 2 * p0 + rows], comp[s].at[q : q + rows], side[k]
                    )
                )
            )

    sent = {}

    def spatial(s):
        for c in crossed[s]:
            c.wait_recv()
        for r in range(4):
            left = jnp.concatenate([tv[s, r, k] for k in range(8)], axis=1)
            right = jnp.concatenate([comp[s][slots[s, r, k]] for k in range(8)], axis=0)
            summed = dot(left, right).astype(jnp.bfloat16)
            hidden = jnp.maximum(dot(summed, weight[...]), 0.0).astype(jnp.bfloat16)
            hid[s, 2 * r : 2 * r + 2] = hidden.reshape(2, 64, 128)
        arr[t * 4 + s] = hid[s, t]
        sent[s] = [
            go(sems.copy(hid.at[s, (t + k) % 8], arr.at[t * 4 + s], times[k]))
            for k in range(1, 8)
        ]

    for s in ORDER:
        share(s, GROUPS[0])
    paired = {}
    for s in EARLY:
        swapped[s].wait_recv()
        paired[s] = ring(pair[s], 1)
    for step in range(1, 5):
        for s in ORDER:
            for c in ringed[s]:
                c.wait_recv()
            if step < 4:
                ringed[s] = ring(own[s], step + 1)
            share(s, GROUPS[step])
        for s in EARLY:
            for c in paired[s]:
                c.wait_recv()
            if step < 4:
                paired[s] = ring(pair[s], step + 1)
            if step == 1:
                keep(pair[s], s, 2, GROUPS[0])
            keep(pair[s], s, 2, GROUPS[step])
        if step == 3:
            for s in LATE:
                swapped[s].wait_recv()
                paired[s] = ring(pair[s], 1)
    for s in LATE:
        keep(pair[s], s, 2, GROUPS[0])
    for step in range(1, 4):
        for s in LATE:
            for c in paired[s]:
                c.wait_recv()
            paired[s] = ring(pair[s], step + 1)
            keep(pair[s], s, 2, GROUPS[step])
    for s in DIRECT + EARLY:
        spatial(s)
    for s in LATE:
        for c in paired[s]:
            c.wait_recv()
        keep(pair[s], s, 2, GROUPS[4])
        spatial(s)
    for s in DIRECT + EARLY + LATE:
        for c in sent[s]:
            c.wait_recv()
        for i in range(4):
            project(8 * i + s, 8 * i + 4 + s, arr, pos, wcat, mix, proj)

    def back(j):
        return pltpu.make_async_remote_copy(
            obuf.at[j], oarr.at[:, t], send.at[sems.n + j], recv.at[sems.n + j],
            device_id=dict(tm=(t + 1 + j) % 8), device_id_type=MESH,
        )

    @pl.loop(0, 3)
    def _(g):
        blocks = [(t + 1 + 2 * g + i) % 8 for i in range(2)]
        for i, tb in enumerate(blocks):
            attend(tb, proj, att, 4 * i)
        obuf[pl.ds(2 * g, 2)] = finish(blocks, att, mix, wout, gain, mlp_up, mlp_down)
        for i in range(2):
            back(2 * g + i).start()

    attend((t + 7) % 8, proj, att)
    obuf[6:7] = finish([(t + 7) % 8], att, mix, wout, gain, mlp_up, mlp_down)
    back(6).start()
    attend(t, proj, att)
    oarr[:, t] = finish([t], att, mix, wout, gain, mlp_up, mlp_down)[0]

    for c in started:
        c.wait_send()

    @pl.loop(0, 7)
    def _(j):
        back(j).wait_recv()

    out[...] = oarr[...]

    @pl.loop(0, 7)
    def _(j):
        back(j).wait_send()

    assert sems.n + 7 == COPIES


def local(
    features, tile_cols, tile_vals, space_weight, positions, attn_proj, attn_out, norm_gain,
    mlp_up, mlp_down,
):
    half, word, single = jnp.bfloat16, jnp.int32, jnp.float32
    block4 = pltpu.VMEM((4, 128, 128), half)
    embedded = pl.pallas_call(
        kernel,
        out_shape=jax.ShapeDtypeStruct((4, 8, 64, 128), half),
        in_specs=[pl.BlockSpec(memory_space=pltpu.HBM)] * 10,
        out_specs=pl.BlockSpec(memory_space=pltpu.VMEM),
        scratch_shapes=[
            pltpu.VMEM((4, 4, 128, 128), half),
            pltpu.VMEM((4, 4, 8), word),
            pltpu.VMEM((4, 4, 8, 128, 128), half),
            pltpu.VMEM((128, 128), half),
            pltpu.VMEM((32, 128), half),
            pltpu.VMEM((128, 384), half),
            pltpu.VMEM((128, 128), half),
            pltpu.VMEM((1, 128), single),
            pltpu.VMEM((128, 512), half),
            pltpu.VMEM((512, 128), half),
            pltpu.VMEM((8, 128), word),
            pltpu.VMEM((4, 8, 128), word),
            pltpu.SMEM((8, 128), word),
            pltpu.SMEM((4, 8, 128), word),
            pltpu.VMEM((3, 8, 128), word),
            pltpu.SMEM((3, 8, 128), word),
            pltpu.VMEM((2 * 4 + len(DIRECT), 16, 128, 128), half),
            pltpu.VMEM((4, 8, 64, 128), half),
            pltpu.VMEM((32, 64, 128), half),
            pltpu.VMEM((192, 256), half),
            pltpu.VMEM((64, 256), half),
            pltpu.VMEM((32, 1, 128), single),
            pltpu.VMEM((32, 64, 128), half),
            pltpu.VMEM((32, 192, 128), single),
            pltpu.VMEM((8, 64, 128), single),
            pltpu.VMEM((7, 4, 64, 128), half),
            pltpu.VMEM((4, 8, 64, 128), half),
            pltpu.SemaphoreType.DMA((COPIES,)),
            pltpu.SemaphoreType.DMA((COPIES,)),
            pltpu.SemaphoreType.DMA((10,)),
        ]
        + [pltpu.VMEM((64, 128, 128), half)] * 4
        + [block4] * 28
        + [block4] * (8 * len(PAIRED)),
        compiler_params=pltpu.CompilerParams(
            collective_id=0, has_side_effects=True, vmem_limit_bytes=44 * 2**20
        ),
    )(
        *[
            pltpu.with_memory_space_constraint(a, pltpu.HBM)
            for a in (
                features.reshape(4, 4, 128, 128), tile_cols, tile_vals, space_weight, positions,
                attn_proj, attn_out, norm_gain.reshape(1, 128), mlp_up, mlp_down,
            )
        ]
    )
    return embedded.reshape(4, 512, 128)


def solution(mesh):
    placed = (
        P("tm", "vert", None),
        P("tm", "vert", None),
        P("tm", "vert", None, None, None),
        P(),
        P(),
        P(),
        P(),
        P(),
        P(),
        P(),
    )
    return jax.shard_map(
        local, mesh=mesh, in_specs=placed, out_specs=P("tm", "vert", None), check_vma=False
    )
```

time: 116 us -> 102 us (0.88)
  Pallas kernels: 111 us -> 101 us
  local copies, waits for them, and re-layouts: 3.24 us -> 0.8 us
    pallas_call x1, Pallas kernels: 111 us -> 101 us  [local(): pl.pallas_call(kernel, out_shape=jax.ShapeDtypeStruct((4, 8, 64, 128), ha...]
where the time goes in v3:
time: 102 us
  Pallas kernels  101 us (99%)
    pallas_call x1, Pallas kernels, local(): pl.pallas_call(kernel, out_shape=jax.ShapeDtypeStruct((4, 8, 64, 128), ha...  101 us

profile of v3, /device:TPU:1, one launch (start us, length us, event | category | flops | bytes accessed | tf_op | source)
XLA Modules:
  0.0 102.1 jit_solution(9970513593428026032)
XLA Ops:
  0.0 101.3 %shard_map.100 = bf16[4,8,64,128]{3,2,1,0:T(8,128)(2,1)S(1)} custom-call(bf16[4,4,128,128]{3,2,1,0:T(8,128)(2,1)} %bitcast.4, s32[4,4,8]{2,1,0:T(4,128)} %cols_h.1, bf16[4,4,8,128,128]{4,3,2,1,0:T(8,128)(2,1)} %tv_h.1, bf16[128,128]{1,0:T(8,128)(2,1)} %weight_h.1, bf16[32,128]{1,0:T(8,128)(2,1)} %positions_h.1, bf16[128,384]{1,0:T(8,128)(2,1)} %attn_proj_h.1, ...), custom_call_target="tpu_custom_call" | custom-call | tf_op jit(solution)/shard_map/pallas_call | solution.py:387
  101.3 0.8 copy.12

commit v4 on v3

--- a/solution.py
+++ b/solution.py
@@ -19,6 +19,7 @@
 DIRECT = (3,)
 EARLY, LATE = (0,), (1, 2)
 ORDER = (3, 0, 1, 2)
+TABLE = {(0, 1): 0, (0, 2): 1, (0, 3): 2, (1, 0): 3, (2, 0): 4, (7, 0): 5, (6, 0): 6}
 
 
 def dot_t(a, b):
@@ -156,20 +157,20 @@
         )
 
 
-COPIES = 3 + 4 * 8 + len(PAIRED) * 9 + 5 * (4 * 2 + len(DIRECT)) + 4 * 7 + 7
+COPIES = len(TABLE) + 4 * 8 + len(PAIRED) * (1 + 4 + 6) + 5 * (4 * 2 + len(DIRECT)) + 4 * 7 + 7
 
 
 def kernel(
     feat_h, cols_h, tv_h, weight_h, positions_h, attn_proj_h, attn_out_h, gain_h, mlp_up_h,
     mlp_down_h, out,
     feat, cols, tv, weight, positions, attn_proj, attn_out, gain, mlp_up, mlp_down,
-    tab_v, slots_v, tab_s, slots, tabr, tabs, stg_refs, hid, arr, wcat, wout, pos, mix, proj, att,
+    tab_v, slots_v, tab_s, slots, tabr, tabs, picked, relay, stg_refs, hid, arr, wcat, wout, pos, mix, proj, att,
     obuf, oarr, send, recv, lsem, *bufs,
 ):
     bufs = list(bufs)
     comp = [bufs.pop(0) for _ in range(4)]
     own = [{dz: bufs.pop(0) for dz in range(1, 8)} for _ in range(4)]
-    pair = {s: {dz: bufs.pop(0) for dz in range(8)} for s in PAIRED}
+    pair = {s: {dz: bufs.pop(0) for dz in (0, 1, 2, 6, 7)} for s in PAIRED}
     for s in range(4):
         own[s][0] = feat.at[s]
     kinds = {s: (1, 3) if s in PAIRED else (1, 3, 2) for s in range(4)}
@@ -181,13 +182,13 @@
     v = lax.axis_index("vert")
     t = lax.axis_index("tm")
     z, x = v // 4, v % 4
-    up = dict(vert=((z + 1) % 8) * 4 + x)
-    down = dict(vert=((z + 7) % 8) * 4 + x)
-    side = {k: dict(vert=z * 4 + (x + k) % 4) for k in (1, 2, 3)}
+    near = {r: dict(vert=((z + r[0]) % 8) * 4 + (x + r[1]) % 4) for r in TABLE}
+    up, down = near[1, 0], near[7, 0]
+    side = {k: near[0, k] for k in (1, 2, 3)}
     times = {k: dict(tm=(t + k) % 8) for k in range(1, 8)}
 
     barrier = pltpu.get_barrier_semaphore()
-    peers = [up, down] + list(side.values()) + list(times.values())
+    peers = list(near.values()) + list(times.values())
     for peer in peers:
         pl.semaphore_signal(barrier, inc=1, device_id=peer, device_id_type=MESH)
 
@@ -201,7 +202,7 @@
             ]
         )
     ]
-    for c in loads:
+    for c in loads[:-1]:
         c.start()
     loads[0].wait()
     index_tables(z, x, cols, tab_v, slots_v)
@@ -225,13 +226,47 @@
             b = sems.copy(buf[3].at[2:4], buf[4].at[2:4], down)
         return go(a), go(b)
 
+    def place(dx, dz):
+        return 2 * (dx * 8 + POS[dz])
+
+    def narrow(s):
+        passed = []
+        for way, to, dz, first, second in ((0, up, 6, (1, 0), (2, 0)), (1, down, 2, (7, 0), (6, 0))):
+            part = picked.at[PAIRED.index(s), way]
+            far = 16 + POS[4] + 32 * way
+            part[2] = pair[s][dz][tabs[TABLE[second], s, far]]
+            end = 16 + POS[5 if way == 0 else 3]
+            for w in range(2):
+                part[w] = pair[s][dz][tabs[TABLE[first], s, 32 * w + end]]
+        for way, to in ((0, up), (1, down)):
+            part = picked.at[PAIRED.index(s), way]
+            passed.append(go(sems.copy(part.at[2:3], relay.at[PAIRED.index(s), way], to)))
+            q = place(2, 5 if way == 0 else 3)
+            narrowed[s].append(go(sems.copy(part.at[0:2], comp[s].at[q : q + 2], to)))
+        return passed
+
+    def last(s):
+        q = place(2, 4)
+        for way, to in ((0, up), (1, down)):
+            narrowed[s].append(
+                go(
+                    sems.copy(
+                        relay.at[PAIRED.index(s), way], comp[s].at[q + way : q + way + 1], to
+                    )
+                )
+            )
+
+    narrowed = {s: [] for s in PAIRED}
     ringed = {}
     ringed[ORDER[0]] = ring(own[ORDER[0]], 1)
-    tables = {k: go(sems.copy(tab_v, tabr.at[3 - k], side[k])) for k in (1, 2, 3)}
+    tables = [
+        go(sems.copy(tab_v, tabr.at[TABLE[(8 - r[0]) % 8, (4 - r[1]) % 4]], near[r]))
+        for r in TABLE
+    ]
     for s in ORDER[1:]:
         ringed[s] = ring(own[s], 1)
     swapped = {s: go(sems.copy(feat.at[s], pair[s][0], side[2])) for s in PAIRED}
-    for c in loads[2:]:
+    for c in loads[2:-1]:
         c.wait()
     mine = [
         pltpu.make_async_copy(tab_v, tab_s, lsem.at[0]),
@@ -243,14 +278,17 @@
     pos[...] = positions[...].astype(jnp.float32).reshape(32, 1, 128)
     for c in mine:
         c.wait()
-    for k in (1, 2, 3):
-        tables[k].wait_recv()
-    theirs = [pltpu.make_async_copy(tabr.at[k], tabs.at[k], lsem.at[2 + k]) for k in range(3)]
+    for c in tables:
+        c.wait_recv()
+    theirs = [
+        pltpu.make_async_copy(tabr.at[k], tabs.at[k], lsem.at[2 + k]) for k in range(len(TABLE))
+    ]
     for c in theirs:
         c.start()
     for c in theirs:
         c.wait()
 
+    loads[-1].start()
     crossed = {s: [] for s in range(4)}
 
     def keep(buf, s, dx, group):
@@ -281,14 +319,15 @@
     sent = {}
 
     def spatial(s):
-        for c in crossed[s]:
+        for c in crossed[s] + narrowed.get(s, []):
             c.wait_recv()
+        summed = []
         for r in range(4):
             left = jnp.concatenate([tv[s, r, k] for k in range(8)], axis=1)
             right = jnp.concatenate([comp[s][slots[s, r, k]] for k in range(8)], axis=0)
-            summed = dot(left, right).astype(jnp.bfloat16)
-            hidden = jnp.maximum(dot(summed, weight[...]), 0.0).astype(jnp.bfloat16)
-            hid[s, 2 * r : 2 * r + 2] = hidden.reshape(2, 64, 128)
+            summed.append(dot(left, right).astype(jnp.bfloat16))
+        hidden = jnp.maximum(dot(jnp.concatenate(summed, axis=0), weight[...]), 0.0)
+        hid[s] = hidden.astype(jnp.bfloat16).reshape(8, 64, 128)
         arr[t * 4 + s] = hid[s, t]
         sent[s] = [
             go(sems.copy(hid.at[s, (t + k) % 8], arr.at[t * 4 + s], times[k]))
@@ -298,9 +337,26 @@
     for s in ORDER:
         share(s, GROUPS[0])
     paired = {}
-    for s in EARLY:
+
+    def begin(s):
         swapped[s].wait_recv()
         paired[s] = ring(pair[s], 1)
+
+    def advance(s, step):
+        for c in paired[s]:
+            c.wait_recv()
+        if step == 1:
+            paired[s] = ring(pair[s], 2)
+            keep(pair[s], s, 2, GROUPS[0])
+        elif step == 2:
+            paired[s] = narrow(s)
+        else:
+            last(s)
+        if step < 3:
+            keep(pair[s], s, 2, GROUPS[step])
+
+    for s in EARLY:
+        begin(s)
     for step in range(1, 5):
         for s in ORDER:
             for c in ringed[s]:
@@ -309,31 +365,18 @@
                 ringed[s] = ring(own[s], step + 1)
             share(s, GROUPS[step])
         for s in EARLY:
-            for c in paired[s]:
-                c.wait_recv()
             if step < 4:
-                paired[s] = ring(pair[s], step + 1)
-            if step == 1:
-                keep(pair[s], s, 2, GROUPS[0])
-            keep(pair[s], s, 2, GROUPS[step])
+                advance(s, step)
         if step == 3:
             for s in LATE:
-                swapped[s].wait_recv()
-                paired[s] = ring(pair[s], 1)
-    for s in LATE:
-        keep(pair[s], s, 2, GROUPS[0])
+                begin(s)
     for step in range(1, 4):
         for s in LATE:
-            for c in paired[s]:
-                c.wait_recv()
-            paired[s] = ring(pair[s], step + 1)
-            keep(pair[s], s, 2, GROUPS[step])
+            advance(s, step)
+    loads[-1].wait()
     for s in DIRECT + EARLY:
         spatial(s)
     for s in LATE:
-        for c in paired[s]:
-            c.wait_recv()
-        keep(pair[s], s, 2, GROUPS[4])
         spatial(s)
     for s in DIRECT + EARLY + LATE:
         for c in sent[s]:
@@ -341,23 +384,27 @@
         for i in range(4):
             project(8 * i + s, 8 * i + 4 + s, arr, pos, wcat, mix, proj)
 
+    def block(j):
+        g = j // 2
+        return (t // 2 + 2 + g + g // 2 + 2 * (g // 3)) % 4 * 2 + (t + j + g // 3) % 2
+
     def back(j):
         return pltpu.make_async_remote_copy(
             obuf.at[j], oarr.at[:, t], send.at[sems.n + j], recv.at[sems.n + j],
-            device_id=dict(tm=(t + 1 + j) % 8), device_id_type=MESH,
+            device_id=dict(tm=block(j)), device_id_type=MESH,
         )
 
     @pl.loop(0, 3)
     def _(g):
-        blocks = [(t + 1 + 2 * g + i) % 8 for i in range(2)]
+        blocks = [block(2 * g + i) for i in range(2)]
         for i, tb in enumerate(blocks):
             attend(tb, proj, att, 4 * i)
         obuf[pl.ds(2 * g, 2)] = finish(blocks, att, mix, wout, gain, mlp_up, mlp_down)
         for i in range(2):
             back(2 * g + i).start()
 
-    attend((t + 7) % 8, proj, att)
-    obuf[6:7] = finish([(t + 7) % 8], att, mix, wout, gain, mlp_up, mlp_down)
+    attend(block(6), proj, att)
+    obuf[6:7] = finish([block(6)], att, mix, wout, gain, mlp_up, mlp_down)
     back(6).start()
     attend(t, proj, att)
     oarr[:, t] = finish([t], att, mix, wout, gain, mlp_up, mlp_down)[0]
@@ -404,8 +451,10 @@
             pltpu.VMEM((4, 8, 128), word),
             pltpu.SMEM((8, 128), word),
             pltpu.SMEM((4, 8, 128), word),
-            pltpu.VMEM((3, 8, 128), word),
-            pltpu.SMEM((3, 8, 128), word),
+            pltpu.VMEM((len(TABLE), 8, 128), word),
+            pltpu.SMEM((len(TABLE), 8, 128), word),
+            pltpu.VMEM((len(PAIRED), 2, 3, 128, 128), half),
+            pltpu.VMEM((len(PAIRED), 2, 1, 128, 128), half),
             pltpu.VMEM((2 * 4 + len(DIRECT), 16, 128, 128), half),
             pltpu.VMEM((4, 8, 64, 128), half),
             pltpu.VMEM((32, 64, 128), half),
@@ -423,7 +472,7 @@
         ]
         + [pltpu.VMEM((64, 128, 128), half)] * 4
         + [block4] * 28
-        + [block4] * (8 * len(PAIRED)),
+        + [block4] * (5 * len(PAIRED)),
         compiler_params=pltpu.CompilerParams(
             collective_id=0, has_side_effects=True, vmem_limit_bytes=44 * 2**20
         ),

time: 102 us -> 97.2 us (0.953)
  Pallas kernels: 101 us -> 96.3 us
    pallas_call x1, Pallas kernels: 101 us -> 96.3 us  [local(): pl.pallas_call(kernel, out_shape=jax.ShapeDtypeStruct((4, 8, 64, 128), ha...]
where the time goes in v4:
time: 97.2 us; the launch traced here: 97.1 us
  Pallas kernels  96.3 us (99%)
    pallas_call x1, Pallas kernels, local(): pl.pallas_call(kernel, out_shape=jax.ShapeDtypeStruct((4, 8, 64, 128), ha...  96.3 us

profile of v4, /device:TPU:1, one launch (start us, length us, event | category | flops | bytes accessed | tf_op | source)
XLA Modules:
  0.0 97.1 jit_solution(3750005921545789662)
XLA Ops:
  0.0 96.3 %shard_map.100 = bf16[4,8,64,128]{3,2,1,0:T(8,128)(2,1)S(1)} custom-call(bf16[4,4,128,128]{3,2,1,0:T(8,128)(2,1)} %bitcast.4, s32[4,4,8]{2,1,0:T(4,128)} %cols_h.1, bf16[4,4,8,128,128]{4,3,2,1,0:T(8,128)(2,1)} %tv_h.1, bf16[128,128]{1,0:T(8,128)(2,1)} %weight_h.1, bf16[32,128]{1,0:T(8,128)(2,1)} %positions_h.1, bf16[128,384]{1,0:T(8,128)(2,1)} %attn_proj_h.1, ...), custom_call_target="tpu_custom_call" | custom-call | tf_op jit(solution)/shard_map/pallas_call | solution.py:434
  96.3 0.8 copy.12

commit v5 on v4

--- a/solution.py
+++ b/solution.py
@@ -157,14 +157,14 @@
         )
 
 
-COPIES = len(TABLE) + 4 * 8 + len(PAIRED) * (1 + 4 + 6) + 5 * (4 * 2 + len(DIRECT)) + 4 * 7 + 7
+COPIES = len(TABLE) + 4 * 8 + len(PAIRED) * (1 + 4 + 4) + 5 * (4 * 2 + len(DIRECT)) + 4 * 7 + 7
 
 
 def kernel(
     feat_h, cols_h, tv_h, weight_h, positions_h, attn_proj_h, attn_out_h, gain_h, mlp_up_h,
     mlp_down_h, out,
     feat, cols, tv, weight, positions, attn_proj, attn_out, gain, mlp_up, mlp_down,
-    tab_v, slots_v, tab_s, slots, tabr, tabs, picked, relay, stg_refs, hid, arr, wcat, wout, pos, mix, proj, att,
+    tab_v, slots_v, tab_s, slots, tabr, tabs, picked, stg_refs, hid, arr, wcat, wout, pos, mix, proj, att,
     obuf, oarr, send, recv, lsem, *bufs,
 ):
     bufs = list(bufs)
@@ -204,8 +204,6 @@
     ]
     for c in loads[:-1]:
         c.start()
-    loads[0].wait()
-    index_tables(z, x, cols, tab_v, slots_v)
     loads[1].wait()
     pl.semaphore_wait(barrier, len(peers))
 
@@ -230,64 +228,56 @@
         return 2 * (dx * 8 + POS[dz])
 
     def narrow(s):
-        passed = []
-        for way, to, dz, first, second in ((0, up, 6, (1, 0), (2, 0)), (1, down, 2, (7, 0), (6, 0))):
+        ends = ((6, (1, 0), (2, 0), 5), (2, (7, 0), (6, 0), 3))
+        for way, (dz, first, second, end) in enumerate(ends):
             part = picked.at[PAIRED.index(s), way]
-            far = 16 + POS[4] + 32 * way
-            part[2] = pair[s][dz][tabs[TABLE[second], s, far]]
-            end = 16 + POS[5 if way == 0 else 3]
+            part[2] = pair[s][dz][tabs[TABLE[second], s, 32 * way + 16 + POS[4]]]
             for w in range(2):
-                part[w] = pair[s][dz][tabs[TABLE[first], s, 32 * w + end]]
-        for way, to in ((0, up), (1, down)):
+                part[w] = pair[s][dz][tabs[TABLE[first], s, 32 * w + 16 + POS[end]]]
+        for way, (dz, first, second, end) in enumerate(ends):
             part = picked.at[PAIRED.index(s), way]
-            passed.append(go(sems.copy(part.at[2:3], relay.at[PAIRED.index(s), way], to)))
-            q = place(2, 5 if way == 0 else 3)
-            narrowed[s].append(go(sems.copy(part.at[0:2], comp[s].at[q : q + 2], to)))
-        return passed
-
-    def last(s):
-        q = place(2, 4)
-        for way, to in ((0, up), (1, down)):
+            q = place(2, 4) + way
             narrowed[s].append(
-                go(
-                    sems.copy(
-                        relay.at[PAIRED.index(s), way], comp[s].at[q + way : q + way + 1], to
-                    )
-                )
+                go(sems.copy(part.at[2:3], comp[s].at[q : q + 1], near[second]))
             )
+            q = place(2, end)
+            narrowed[s].append(go(sems.copy(part.at[0:2], comp[s].at[q : q + 2], near[first])))
 
     narrowed = {s: [] for s in PAIRED}
-    ringed = {}
-    ringed[ORDER[0]] = ring(own[ORDER[0]], 1)
-    tables = [
-        go(sems.copy(tab_v, tabr.at[TABLE[(8 - r[0]) % 8, (4 - r[1]) % 4]], near[r]))
-        for r in TABLE
-    ]
+    ringed = {ORDER[0]: ring(own[ORDER[0]], 1)}
+    loads[0].wait()
+    index_tables(z, x, cols, tab_v, slots_v)
+
+    def tell(r):
+        return go(sems.copy(tab_v, tabr.at[TABLE[(8 - r[0]) % 8, (4 - r[1]) % 4]], near[r]))
+
+    def hear(tables, held):
+        for c in tables:
+            c.wait_recv()
+        held = [pltpu.make_async_copy(tabr.at[k], tabs.at[k], lsem.at[2 + k]) for k in held]
+        for c in held:
+            c.start()
+        for c in held:
+            c.wait()
+
+    sideways = [tell(r) for r in TABLE if r[1]]
+    swapped = {s: go(sems.copy(feat.at[s], pair[s][0], side[2])) for s in PAIRED}
     for s in ORDER[1:]:
         ringed[s] = ring(own[s], 1)
-    swapped = {s: go(sems.copy(feat.at[s], pair[s][0], side[2])) for s in PAIRED}
-    for c in loads[2:-1]:
-        c.wait()
+    along = [tell(r) for r in TABLE if r[0]]
     mine = [
         pltpu.make_async_copy(tab_v, tab_s, lsem.at[0]),
         pltpu.make_async_copy(slots_v, slots, lsem.at[1]),
     ]
+    for c in loads[2:-1]:
+        c.wait()
     for c in mine:
         c.start()
     arrange(attn_proj, attn_out, wcat, wout)
     pos[...] = positions[...].astype(jnp.float32).reshape(32, 1, 128)
     for c in mine:
         c.wait()
-    for c in tables:
-        c.wait_recv()
-    theirs = [
-        pltpu.make_async_copy(tabr.at[k], tabs.at[k], lsem.at[2 + k]) for k in range(len(TABLE))
-    ]
-    for c in theirs:
-        c.start()
-    for c in theirs:
-        c.wait()
-
+    hear(sideways, range(3))
     loads[-1].start()
     crossed = {s: [] for s in range(4)}
 
@@ -322,17 +312,23 @@
         for c in crossed[s] + narrowed.get(s, []):
             c.wait_recv()
         summed = []
-        for r in range(4):
+        far = [(t // 2 + k) % 4 for k in (2, 1, 3, 0)]
+        for r in far:
             left = jnp.concatenate([tv[s, r, k] for k in range(8)], axis=1)
             right = jnp.concatenate([comp[s][slots[s, r, k]] for k in range(8)], axis=0)
             summed.append(dot(left, right).astype(jnp.bfloat16))
-        hidden = jnp.maximum(dot(jnp.concatenate(summed, axis=0), weight[...]), 0.0)
-        hid[s] = hidden.astype(jnp.bfloat16).reshape(8, 64, 128)
+        for i in range(4):
+            hidden = jnp.maximum(dot(summed[i], weight[...]), 0.0).astype(jnp.bfloat16)
+            hid[s, pl.ds(2 * far[i], 2)] = hidden.reshape(2, 64, 128)
         arr[t * 4 + s] = hid[s, t]
-        sent[s] = [
-            go(sems.copy(hid.at[s, (t + k) % 8], arr.at[t * 4 + s], times[k]))
-            for k in range(1, 8)
-        ]
+        sent[s] = []
+        for i, k in enumerate((2, 1, 3, 0)):
+            for core in range(2):
+                if k or core:
+                    peer = far[i] * 2 + (t + core) % 2
+                    sent[s].append(
+                        go(sems.copy(hid.at[s, peer], arr.at[t * 4 + s], dict(tm=peer)))
+                    )
 
     for s in ORDER:
         share(s, GROUPS[0])
@@ -348,12 +344,9 @@
         if step == 1:
             paired[s] = ring(pair[s], 2)
             keep(pair[s], s, 2, GROUPS[0])
-        elif step == 2:
-            paired[s] = narrow(s)
         else:
-            last(s)
-        if step < 3:
-            keep(pair[s], s, 2, GROUPS[step])
+            narrow(s)
+        keep(pair[s], s, 2, GROUPS[step])
 
     for s in EARLY:
         begin(s)
@@ -365,12 +358,14 @@
                 ringed[s] = ring(own[s], step + 1)
             share(s, GROUPS[step])
         for s in EARLY:
-            if step < 4:
+            if step < 3:
                 advance(s, step)
+        if step == 1:
+            hear(along, range(3, 7))
         if step == 3:
             for s in LATE:
                 begin(s)
-    for step in range(1, 4):
+    for step in range(1, 3):
         for s in LATE:
             advance(s, step)
     loads[-1].wait()
@@ -378,11 +373,21 @@
         spatial(s)
     for s in LATE:
         spatial(s)
-    for s in DIRECT + EARLY + LATE:
+    for s in DIRECT + EARLY + LATE[:1]:
         for c in sent[s]:
             c.wait_recv()
-        for i in range(4):
-            project(8 * i + s, 8 * i + 4 + s, arr, pos, wcat, mix, proj)
+
+    @pl.loop(0, 4)
+    def _(i):
+        s = (3 + i) % 4
+
+        @pl.when(i == 3)
+        def _():
+            for c in sent[2]:
+                c.wait_recv()
+
+        for k in range(4):
+            project(8 * k + s, 8 * k + 4 + s, arr, pos, wcat, mix, proj)
 
     def block(j):
         g = j // 2
@@ -403,11 +408,16 @@
         for i in range(2):
             back(2 * g + i).start()
 
-    attend(block(6), proj, att)
-    obuf[6:7] = finish([block(6)], att, mix, wout, gain, mlp_up, mlp_down)
-    back(6).start()
-    attend(t, proj, att)
-    oarr[:, t] = finish([t], att, mix, wout, gain, mlp_up, mlp_down)[0]
+    @pl.loop(6, 8)
+    def _(j):
+        attend(block(j), proj, att)
+        obuf[pl.ds(j, 1)] = finish([block(j)], att, mix, wout, gain, mlp_up, mlp_down)
+
+        @pl.when(j == 6)
+        def _():
+            back(6).start()
+
+    oarr[:, t] = obuf[7]
 
     for c in started:
         c.wait_send()
@@ -454,7 +464,6 @@
             pltpu.VMEM((len(TABLE), 8, 128), word),
             pltpu.SMEM((len(TABLE), 8, 128), word),
             pltpu.VMEM((len(PAIRED), 2, 3, 128, 128), half),
-            pltpu.VMEM((len(PAIRED), 2, 1, 128, 128), half),
             pltpu.VMEM((2 * 4 + len(DIRECT), 16, 128, 128), half),
             pltpu.VMEM((4, 8, 64, 128), half),
             pltpu.VMEM((32, 64, 128), half),
@@ -463,8 +472,8 @@
             pltpu.VMEM((32, 1, 128), single),
             pltpu.VMEM((32, 64, 128), half),
             pltpu.VMEM((32, 192, 128), single),
-            pltpu.VMEM((8, 64, 128), single),
-            pltpu.VMEM((7, 4, 64, 128), half),
+            pltpu.VMEM((16, 64, 128), single),
+            pltpu.VMEM((8, 4, 64, 128), half),
             pltpu.VMEM((4, 8, 64, 128), half),
             pltpu.SemaphoreType.DMA((COPIES,)),
             pltpu.SemaphoreType.DMA((COPIES,)),

time: 97.2 us -> 96.2 us (0.990)
  Pallas kernels: 96.3 us -> 95.3 us
    pallas_call x1, Pallas kernels: 96.3 us -> 95.3 us  [local(): pl.pallas_call(kernel, out_shape=jax.ShapeDtypeStruct((4, 8, 64, 128), ha...]
where the time goes in v5:
time: 96.2 us; the launch traced here: 96.1 us
  Pallas kernels  95.3 us (99%)
    pallas_call x1, Pallas kernels, local(): pl.pallas_call(kernel, out_shape=jax.ShapeDtypeStruct((4, 8, 64, 128), ha...  95.3 us

profile of v5, /device:TPU:1, one launch (start us, length us, event | category | flops | bytes accessed | tf_op | source)
XLA Modules:
  0.0 96.1 jit_solution(17599064359175492391)
XLA Ops:
  0.0 95.3 %shard_map.100 = bf16[4,8,64,128]{3,2,1,0:T(8,128)(2,1)S(1)} custom-call(bf16[4,4,128,128]{3,2,1,0:T(8,128)(2,1)} %bitcast.4, s32[4,4,8]{2,1,0:T(4,128)} %cols_h.1, bf16[4,4,8,128,128]{4,3,2,1,0:T(8,128)(2,1)} %tv_h.1, bf16[128,128]{1,0:T(8,128)(2,1)} %weight_h.1, bf16[32,128]{1,0:T(8,128)(2,1)} %positions_h.1, bf16[128,384]{1,0:T(8,128)(2,1)} %attn_proj_h.1, ...), custom_call_target="tpu_custom_call" | custom-call | tf_op jit(solution)/shard_map/pallas_call | solution.py:444
  95.3 0.8 copy.12

commit v6 on v5

--- a/solution.py
+++ b/solution.py
@@ -93,12 +93,14 @@
 
 def finish(blocks, att, mix, wout, gain, mlp_up, mlp_down):
     n = 4 * len(blocks)
-    rows = jnp.concatenate([att[i].T for i in range(n)], axis=0).astype(jnp.bfloat16)
-    o = dot(rows, wout[...])
-    out = jnp.concatenate(
-        [o[128 * i : 128 * i + 64, 0:128] + o[128 * i + 64 : 128 * i + 128, 128:256] for i in range(n)],
-        axis=0,
-    )
+    out = []
+    for i in range(n):
+        o = lax.dot_general(
+            att[i].astype(jnp.bfloat16), wout[...], (((0,), (0,)), ((), ())),
+            preferred_element_type=jnp.float32,
+        )
+        out.append(o[0:64, 0:128] + o[64:128, 128:256])
+    out = jnp.concatenate(out, axis=0)
     m = jnp.concatenate([mix[pl.ds(4 * tb, 4)].reshape(256, 128) for tb in blocks], axis=0)
     stream = m.astype(jnp.float32) + out
     centre = jnp.mean(stream, axis=-1, keepdims=True)
@@ -245,6 +247,11 @@
 
     narrowed = {s: [] for s in PAIRED}
     ringed = {ORDER[0]: ring(own[ORDER[0]], 1)}
+
+    def swap(s):
+        return go(sems.copy(feat.at[s], pair[s][0], side[2]))
+
+    swapped = {PAIRED[0]: swap(PAIRED[0])}
     loads[0].wait()
     index_tables(z, x, cols, tab_v, slots_v)
 
@@ -261,7 +268,7 @@
             c.wait()
 
     sideways = [tell(r) for r in TABLE if r[1]]
-    swapped = {s: go(sems.copy(feat.at[s], pair[s][0], side[2])) for s in PAIRED}
+    swapped |= {s: swap(s) for s in PAIRED[1:]}
     for s in ORDER[1:]:
         ringed[s] = ring(own[s], 1)
     along = [tell(r) for r in TABLE if r[0]]
@@ -311,24 +318,26 @@
     def spatial(s):
         for c in crossed[s] + narrowed.get(s, []):
             c.wait_recv()
-        summed = []
         far = [(t // 2 + k) % 4 for k in (2, 1, 3, 0)]
-        for r in far:
-            left = jnp.concatenate([tv[s, r, k] for k in range(8)], axis=1)
-            right = jnp.concatenate([comp[s][slots[s, r, k]] for k in range(8)], axis=0)
-            summed.append(dot(left, right).astype(jnp.bfloat16))
-        for i in range(4):
-            hidden = jnp.maximum(dot(summed[i], weight[...]), 0.0).astype(jnp.bfloat16)
-            hid[s, pl.ds(2 * far[i], 2)] = hidden.reshape(2, 64, 128)
+        sent[s] = []
+        for part in ((0, 1), (2, 3)):
+            summed = []
+            for i in part:
+                r = far[i]
+                left = jnp.concatenate([tv[s, r, k] for k in range(8)], axis=1)
+                right = jnp.concatenate([comp[s][slots[s, r, k]] for k in range(8)], axis=0)
+                summed.append(dot(left, right).astype(jnp.bfloat16))
+            for i, rows in zip(part, summed):
+                hidden = jnp.maximum(dot(rows, weight[...]), 0.0).astype(jnp.bfloat16)
+                hid[s, pl.ds(2 * far[i], 2)] = hidden.reshape(2, 64, 128)
+            for i in part:
+                for core in range(2):
+                    if i < 3 or core:
+                        peer = far[i] * 2 + (t + core) % 2
+                        sent[s].append(
+                            go(sems.copy(hid.at[s, peer], arr.at[t * 4 + s], dict(tm=peer)))
+                        )
         arr[t * 4 + s] = hid[s, t]
-        sent[s] = []
-        for i, k in enumerate((2, 1, 3, 0)):
-            for core in range(2):
-                if k or core:
-                    peer = far[i] * 2 + (t + core) % 2
-                    sent[s].append(
-                        go(sems.copy(hid.at[s, peer], arr.at[t * 4 + s], dict(tm=peer)))
-                    )
 
     for s in ORDER:
         share(s, GROUPS[0])
@@ -373,7 +382,7 @@
         spatial(s)
     for s in LATE:
         spatial(s)
-    for s in DIRECT + EARLY + LATE[:1]:
+    for s in DIRECT + EARLY + LATE[:-1]:
         for c in sent[s]:
             c.wait_recv()
 

time: 96.2 us -> 95.8 us (level)
  no operation moved by 1% of the time
where the time goes in v6:
time: 95.8 us; the launch traced here: 95.7 us
  Pallas kernels  94.9 us (99%)
    pallas_call x1, Pallas kernels, local(): pl.pallas_call(kernel, out_shape=jax.ShapeDtypeStruct((4, 8, 64, 128), ha...  94.9 us

profile of v6, /device:TPU:1, one launch (start us, length us, event | category | flops | bytes accessed | tf_op | source)
XLA Modules:
  0.0 95.7 jit_solution(10958388205301364011)
XLA Ops:
  0.0 94.9 %shard_map.100 = bf16[4,8,64,128]{3,2,1,0:T(8,128)(2,1)S(1)} custom-call(bf16[4,4,128,128]{3,2,1,0:T(8,128)(2,1)} %bitcast.4, s32[4,4,8]{2,1,0:T(4,128)} %cols_h.1, bf16[4,4,8,128,128]{4,3,2,1,0:T(8,128)(2,1)} %tv_h.1, bf16[128,128]{1,0:T(8,128)(2,1)} %weight_h.1, bf16[32,128]{1,0:T(8,128)(2,1)} %positions_h.1, bf16[128,384]{1,0:T(8,128)(2,1)} %attn_proj_h.1, ...), custom_call_target="tpu_custom_call" | custom-call | tf_op jit(solution)/shard_map/pallas_call | solution.py:453
  94.9 0.8 copy.12

commit v7 on v6

--- a/solution.py
+++ b/solution.py
@@ -371,9 +371,8 @@
                 advance(s, step)
         if step == 1:
             hear(along, range(3, 7))
-        if step == 3:
-            for s in LATE:
-                begin(s)
+        if step in (2, 3):
+            begin(LATE[step - 2])
     for step in range(1, 3):
         for s in LATE:
             advance(s, step)

time: 95.8 us -> 95.8 us (level)
  no operation moved by 1% of the time
where the time goes in v7:
time: 95.8 us; the launch traced here: 95.7 us
  Pallas kernels  94.9 us (99%)
    pallas_call x1, Pallas kernels, local(): pl.pallas_call(kernel, out_shape=jax.ShapeDtypeStruct((4, 8, 64, 128), ha...  94.9 us

profile of v7, /device:TPU:1, one launch (start us, length us, event | category | flops | bytes accessed | tf_op | source)
XLA Modules:
  0.0 95.7 jit_solution(785059972019759630)
XLA Ops:
  0.0 94.9 %shard_map.100 = bf16[4,8,64,128]{3,2,1,0:T(8,128)(2,1)S(1)} custom-call(bf16[4,4,128,128]{3,2,1,0:T(8,128)(2,1)} %bitcast.4, s32[4,4,8]{2,1,0:T(4,128)} %cols_h.1, bf16[4,4,8,128,128]{4,3,2,1,0:T(8,128)(2,1)} %tv_h.1, bf16[128,128]{1,0:T(8,128)(2,1)} %weight_h.1, bf16[32,128]{1,0:T(8,128)(2,1)} %positions_h.1, bf16[128,384]{1,0:T(8,128)(2,1)} %attn_proj_h.1, ...), custom_call_target="tpu_custom_call" | custom-call | tf_op jit(solution)/shard_map/pallas_call | solution.py:452
  94.9 0.8 copy.12
